TPU v7x, 128 devices: a whole 4x4x4 slice. The times are simulated.
128 devices in a mesh: replica: 2 (over core), shard: 64 (over z, y, x).
Axes of the slice: x: 4, y: 4, z: 4, core: 2. Of those that a mesh axis runs over, the one named last changes fastest.
Arguments:
- dense_input: bfloat16 [16384, 256], P(('replica', 'shard')), may hold values from -6 to 6
- bag_rows: int32 [16384, 2, 16], P(('replica', 'shard')), may hold values from 0 to 32767, as said below
- bag_lengths: int32 [16384, 2], P(('replica', 'shard')), may hold values from 1 to 16
- bag_weights: bfloat16 [16384, 2, 16], P(('replica', 'shard')), may hold values from 0.5 to 2
- labels: int32 [16384], P(('replica', 'shard')), may hold values 0 or 1
- embedding: float32 [32768, 2, 256], P('shard'), may hold values from -2 to 2
- first_moment: float32 [32768, 2, 256], P('shard'), may hold values from -6 to 6
- second_moment: float32 [32768, 2], P('shard'), may hold values from 0.5 to 8
- cross_weight: bfloat16 [768, 768], replicated, may hold values from -0.21875 to 0.21875
- hidden_weight: bfloat16 [768, 4096], replicated, may hold values from -0.21875 to 0.21875
- head_weight: bfloat16 [4096], replicated, may hold values from -0.09375 to 0.09375
Outputs:
- new_first: float32 [32768, 2, 256], P('shard')
- new_second: float32 [32768, 2], P('shard')
- row_step: float32 [32768, 2, 256], P('shard')
Inputs may be any that keep to these rules, and one draw needn't show every extreme that they name: `bag_rows`: call the rows k * 512 to (k + 1) * 512 - 1 those of owner k. For each table, all slots of one device's 128 samples (used or not) name at most 32 distinct rows of any one owner, and every device names exactly 32 distinct rows of some owner in each table. Row indices may be held and sent in any lossless form.
All inputs are finite; a program needn't handle non-finite values. No bound on the sum of `labels` on one device may be relied on, other than what follows from the above.
Results may differ from a plain program's by a relative error of at most 0.0038.
The roundings to bfloat16 on the way count: a program that leaves them out, or rounds other values in their place, can miss the bound.
Values may be sent and summed in bfloat16 or wider, within the bound.
No kernel may reach another device: no remote copies, remote signals or barrier semaphores. Data moves between devices by JAX's collectives and lax.ppermute only.
A program may use at most 128 MiB of HBM per device.

v0:
```python
import jax
import jax.numpy as jnp
from jax import lax
from jax.sharding import PartitionSpec as P

loss_scale = 64.0
beta_first = 0.9
beta_second = 0.99
epsilon = 1e-08


def dense_pass(dense_part, pooled, marks, cross_weight, hidden_weight, head_weight):
    samples = dense_part.shape[0]
    joined = jnp.concatenate(
        [dense_part.astype(jnp.float32), pooled.reshape(samples, -1)], axis=1
    ).astype(jnp.bfloat16)
    widened = joined.astype(jnp.float32)
    crossed = jnp.dot(joined, cross_weight, preferred_element_type=jnp.float32)
    layered = (widened * crossed + widened).astype(jnp.bfloat16)
    before = jnp.dot(layered, hidden_weight, preferred_element_type=jnp.float32)
    hidden = jnp.maximum(before, 0.0).astype(jnp.bfloat16)
    logits = jnp.dot(hidden, head_weight, preferred_element_type=jnp.float32)
    slope = (jax.nn.sigmoid(logits) - marks.astype(jnp.float32)) * loss_scale
    back_hidden = jnp.where(
        before > 0.0, slope[:, None] * head_weight.astype(jnp.float32)[None, :], 0.0
    ).astype(jnp.bfloat16)
    back_layered = lax.dot_general(
        back_hidden, hidden_weight, (((1,), (1,)), ((), ())), preferred_element_type=jnp.float32
    )
    mixed = (back_layered * widened).astype(jnp.bfloat16)
    back_joined = back_layered * (crossed + 1.0) + lax.dot_general(
        mixed, cross_weight, (((1,), (1,)), ((), ())), preferred_element_type=jnp.float32
    )
    return back_joined[:, dense_part.shape[1] :].reshape(pooled.shape).astype(jnp.bfloat16)


def adam_rows(row_grad, hits, first_moment, second_moment):
    touched = hits > 0.0
    first_new = jnp.where(
        touched[:, :, None], beta_first * first_moment + (1.0 - beta_first) * row_grad, first_moment
    )
    second_new = jnp.where(
        touched,
        beta_second * second_moment + (1.0 - beta_second) * jnp.mean(row_grad * row_grad, axis=2),
        second_moment,
    )
    step = jnp.where(
        touched[:, :, None], first_new / (jnp.sqrt(second_new)[:, :, None] + epsilon), 0.0
    )
    return (first_new, second_new, step)


def slot_masses(bag_lengths, bag_weights):
    slots = bag_weights.shape[2]
    usable = jnp.arange(slots, dtype=jnp.int32)[None, None, :] < bag_lengths[:, :, None]
    return (jnp.where(usable, bag_weights, jnp.zeros_like(bag_weights)), usable)


def slot_counts(bags, masses, first_row, columns_total):
    columns = jnp.arange(columns_total, dtype=jnp.int32)
    local_ids = bags - first_row
    counts = jnp.zeros((bags.shape[0], bags.shape[1], columns_total), jnp.float32)
    for slot in range(bags.shape[2]):
        matches = local_ids[:, :, slot, None] == columns
        counts = counts + jnp.where(matches, masses[:, :, slot, None].astype(jnp.float32), 0.0)
    return counts


def local(
    dense_input,
    bag_rows,
    bag_lengths,
    bag_weights,
    labels,
    embedding,
    first_moment,
    second_moment,
    cross_weight,
    hidden_weight,
    head_weight,
):
    own_rows = embedding.shape[0]
    first_row = lax.axis_index("shard") * own_rows
    embedding_low = embedding.astype(jnp.bfloat16)
    masked_low, usable = slot_masses(bag_lengths, bag_weights)
    group_bags, group_masses = (
        lax.all_gather(bag_rows, "shard", axis=0, tiled=True),
        lax.all_gather(masked_low, "shard", axis=0, tiled=True),
    )
    group_counts = slot_counts(group_bags, group_masses, first_row, own_rows)
    hits = jnp.transpose(jnp.sum(group_counts, axis=0))
    group_low = group_counts.astype(jnp.bfloat16)
    block = group_low
    pooled = lax.psum_scatter(
        jnp.einsum("gtr,rte->gte", block, embedding_low, preferred_element_type=jnp.float32),
        "shard",
        scatter_dimension=0,
        tiled=True,
    )
    bag_grads = dense_pass(dense_input, pooled, labels, cross_weight, hidden_weight, head_weight)
    block = group_low
    row_grad = jnp.einsum(
        "gtr,gte->rte",
        block,
        lax.all_gather(bag_grads, "shard", axis=0, tiled=True),
        preferred_element_type=jnp.float32,
    )
    first_new, second_new, step = adam_rows(row_grad, hits, first_moment, second_moment)
    summed = lax.psum((first_new, second_new, step), "replica")
    replicas = lax.axis_size("replica")
    return (summed[0] / replicas, summed[1] / replicas, summed[2] / replicas)


def solution(mesh):
    placed = (
        P(("replica", "shard"), None),
        P(("replica", "shard"), None, None),
        P(("replica", "shard"), None),
        P(("replica", "shard"), None, None),
        P(("replica", "shard")),
        P("shard", None, None),
        P("shard", None, None),
        P("shard", None),
        P(),
        P(),
        P(),
    )
    return jax.shard_map(
        local,
        mesh=mesh,
        in_specs=placed,
        out_specs=(P("shard", None, None), P("shard", None), P("shard", None, None)),
        check_vma=False,
    )
```

profile of v0, /device:TPU:1, one launch (start us, length us, event | category | flops | bytes accessed | tf_op | source)
XLA Modules:
  0.0 827.7 jit_solution(9956745195978551686)
XLA Ops:
  7.2 0.7 all-gather.3.cloned.1.call-update
  8.0 0.7 fusion.24
  8.7 153.7 %all_gather.10 = bf16[8192,2,16]{0,2,1:T(8,128)(2,1)S(1)} all-gather(bf16[128,2,16]{0,2,1:T(8,128)(2,1)S(1)} %fusion.24), channel_id=1, replica_groups=mesh['replica'=2,'shard'=64] {'shard'}, dimensions={0}, use_global_device_ids=true | all-gather | bytes 532480 | tf_op jit(solution)/shard_map/all_gather | solution.py:88
  162.4 1.1 slice_convert_fusion.15
  163.5 0.1 copy_bitcast_fusion.4
  163.6 0.1 copy_bitcast_fusion.8
  163.7 0.1 copy_bitcast_fusion.12
  163.8 0.1 copy_bitcast_fusion.16
  163.9 0.1 copy_bitcast_fusion.20
  164.0 0.1 copy_bitcast_fusion.24
  164.1 0.1 copy_bitcast_fusion.28
  164.3 1.6 convert_element_type.22
  165.9 0.1 copy_bitcast_fusion
  166.0 1.3 broadcast_subtract_fusion
  167.3 1.0 fusion.34
  168.3 0.1 copy_bitcast_fusion.9
  168.4 0.1 copy_bitcast_fusion.13
  168.5 0.1 copy_bitcast_fusion.17
  168.6 0.1 copy_bitcast_fusion.21
  168.8 0.1 copy_bitcast_fusion.25
  168.9 0.1 copy_bitcast_fusion.29
  169.0 0.1 copy_bitcast_fusion.5
  169.1 0.1 copy_bitcast_fusion.1
  169.2 76.3 %fusion.33 = (f32[2,512]{1,0:T(2,128)S(1)}, bf16[8192,2,512]{2,0,1:T(8,128)(2,1)}) fusion(f32[8192,2]{0,1:T(2,128)S(1)} %get-tuple-element.52, s32[8192,2]{0,1:T(2,128)S(1)} %get-tuple-element.68, f32[8192,2]{0,1:T(2,128)S(1)} %get-tuple-element.53, s32[8192,2]{0,1:T(2,128)S(1)} %get-tuple-element.69, f32[8192,2]{0,1:T(2,128)S(1)} %get-tuple-element.54, ...), kind=kLoop, calls=%fused_computation.115 | loop fusion | flops 411040768 | bytes 18878464 | tf_op jit(solution)/shard_map/reduce_sum | solution.py:91
  245.5 16.0 %convolution_bitcast_fusion = f32[8192,2,256]{2,0,1:T(8,128)} fusion(bf16[8192,2,512]{2,0,1:T(8,128)(2,1)} %get-tuple-element.17, bf16[512,2,256]{2,1,0:T(2,128)(2,1)S(1)} %convert_element_type.22), kind=kOutput, calls=%fused_computation.17 | convolution fusion | flops 4294967296 | bytes 34078720 | tf_op jit(solution)/shard_map/gtr,rte->gte/dot_general | solution.py:95
  261.6 0.2 all-gather.5.cloned.1.call-start
  261.9 0.4 copy-done.2
  262.3 360.7 %reduce-scatter.2.cloned.1.call-done = f32[128,2,256]{2,0,1:T(8,128)} async-done(((f32[8192,2,256]{2,0,1:T(8,128)}), f32[128,2,256]{2,0,1:T(8,128)}) %reduce-scatter.2.cloned.1.call-update) | async-done | bytes 262160 | tf_op jit(solution)/shard_map/reduce_scatter | solution.py:94
  623.0 1.0 convert.24
  624.0 0.8 copy.22
  624.8 1.0 copy.23
  625.8 0.3 fusion.23
  626.1 3.9 fusion.19
  630.1 0.4 fusion.8
  630.5 2.2 fusion.9
  632.7 0.5 fusion.21
  633.3 0.8 copy.28
  634.2 1.5 copy.20
  635.7 140.4 %all-gather.5.cloned.1.call-done = bf16[8192,2,256]{0,2,1:T(8,128)(2,1)} async-done(((bf16[128,2,256]{0,2,1:T(8,128)(2,1)}), bf16[8192,2,256]{0,2,1:T(8,128)(2,1)}) %all-gather.5.cloned.1.call-update) | async-done | bytes 8388624 | tf_op jit(solution)/shard_map/all_gather | solution.py:105
  776.1 10.5 %multiply_reduce_fusion = (f32[2,512]{1,0:T(2,128)S(1)}, f32[2,256,512]{2,1,0:T(8,128)S(1)}) fusion(bf16[8192,2,256]{0,2,1:T(8,128)(2,1)} %all-gather.5.cloned.1.call-done, bf16[8192,2,512]{2,0,1:T(8,128)(2,1)} %get-tuple-element.17), kind=kOutput, calls=%fused_computation.34 | convolution fusion | flops 4295490560 | bytes 26218496 | tf_op jit(solution)/shard_map/gtr,gte->rte/dot_general | solution.py:102
  786.6 1.6 divide_select_fusion
  788.3 3.7 psum.22
  792.0 0.6 broadcast_multiply_fusion.2
  792.6 23.3 %all-reduce.3.cloned.1.call-done = (f32[512,2,256]{0,2,1:T(8,128)}, f32[512,2,256]{0,2,1:T(8,128)}) async-done(((f32[512,2,256]{0,2,1:T(8,128)}, f32[512,2,256]{0,2,1:T(8,128)}), (f32[512,2,256]{0,2,1:T(8,128)}, f32[512,2,256]{0,2,1:T(8,128)})) %all-reduce.3.cloned.1.call-update) | async-done | bytes 2097168 | tf_op jit(solution)/shard_map/psum | solution.py:109
  815.9 1.3 broadcast_multiply_fusion.1
  817.2 1.3 copy.26
  818.5 1.3 broadcast_multiply_fusion
  819.8 1.3 copy.27
  (25 shorter events, 0.3 us)
Async XLA Ops:
  7.2 618.6 %copy-start = (bf16[768,768]{1,0:T(8,128)(2,1)S(1)}, bf16[768,768]{1,0:T(8,128)(2,1)}, u32[]{:S(2)}) copy-start(bf16[768,768]{1,0:T(8,128)(2,1)} %param.19) | copy-start | bytes 3538948
  7.2 158.8 %all-gather.3.cloned.1.call-start = ((), (), s32[]{:S(2)}) async-start(), calls=%async_computation.1 | async-start | bytes 1064960 | tf_op jit(solution)/shard_map/all_gather | solution.py:87
  7.9 615.1 %reduce-scatter.2.cloned.1.call-start = ((), (), s32[]{:S(2)}) async-start(), calls=%async_computation.2 | async-start | bytes 17039360 | tf_op jit(solution)/shard_map/reduce_scatter | solution.py:94
  261.6 0.7 copy-start.2
  261.6 364.2 %copy-start.1 = (bf16[128,256]{1,0:T(8,128)(2,1)S(1)}, bf16[128,256]{1,0:T(8,128)(2,1)}, u32[]{:S(2)}) copy-start(bf16[128,256]{1,0:T(8,128)(2,1)} %param.11) | copy-start | bytes 196612
  261.6 368.5 %copy-start.4 = (s32[128]{0:T(128)S(1)}, s32[128]{0:T(128)}, u32[]{:S(2)}) copy-start(s32[128]{0:T(128)} %param.15) | copy-start | bytes 1540
  261.6 368.9 %slice-start = ((s8[6291456]{0:T(1024)(128)(4,1)}), s8[2097152]{0:T(1024)(128)(4,1)S(1)}, s32[]{:S(2)}) async-start(s8[6291456]{0:T(1024)(128)(4,1)} %bitcast.103), calls=%async_computation.5 | async-start | bytes 4194304
  261.6 514.4 %all-gather.5.cloned.1.call-start = ((), (), s32[]{:S(2)}) async-start(), calls=%async_computation.3 | async-start | bytes 8519680 | tf_op jit(solution)/shard_map/all_gather | solution.py:105
  626.1 4.4 slice-start.1
  634.1 181.7 %all-reduce.3.cloned.1.call-start = ((), (), s32[]{:S(2)}) async-start(), calls=%async_computation.4 | async-start | bytes 4194304 | tf_op jit(solution)/shard_map/psum | solution.py:109
  635.7 150.9 %copy-start.3 = (f32[512,2]{0,1:T(2,128)S(1)}, f32[512,2]{0,1:T(2,128)}, u32[]{:S(2)}) copy-start(f32[512,2]{0,1:T(2,128)} %param.18) | copy-start | bytes 12292
Sparse Core Ops, SparseCore 0:
  10.7 65.5 all-gather.2
  261.7 361.2 reduce-scatter.1
  634.2 141.7 all-gather.4
  788.4 27.4 all-reduce.2
where the time goes:
time: 828 us
  waiting for transfers between devices  525 us (63%)
  blocking collectives  157 us (19%)
  other arithmetic  86.9 us (10%)
  matrix products  34 us (4%)
  between operations  14.1 us (2%)
  local copies, waits for them, and re-layouts  9.75 us (1%)
    reduce_scatter x1, waiting for transfers between devices, local(): lax.psum_scatter(jnp.einsum('gtr,rte->gte', block, embedding_low, preferr...  361 us
    all_gather x1, blocking collectives, local(): lax.all_gather(masked_low, 'shard', axis=0, tiled=True)  154 us
    all_gather x1, waiting for transfers between devices, local(): lax.all_gather(bag_grads, 'shard', axis=0, tiled=True)  140 us
    reduce_sum x1, other arithmetic, local(): hits = jnp.transpose(jnp.sum(group_counts, axis=0))  76.3 us
    psum x1, waiting for transfers between devices, local(): summed = lax.psum((first_new, second_new, step), 'replica')  23.3 us
  transfers between devices with their start and end apart: 4, of which 3 were waited for; matrix products, arithmetic and copies ran while one was open for 1% of the time, Pallas kernels for 0%

commit v1 on v0

v1 whole, which is shorter than its diff:
```python
import functools

import jax
import jax.numpy as jnp
from jax import lax
from jax.experimental import pallas as pl
from jax.experimental.pallas import tpu as pltpu
from jax.sharding import PartitionSpec as P

loss_scale = 64.0
beta_first = 0.9
beta_second = 0.99
epsilon = 1e-08

CAP = 32
LANES = 128
UNTOUCHED = 1e30
F32 = jnp.float32
BF16 = jnp.bfloat16
VMEM_LIMIT = 56 * 1024 * 1024

NN = (((1,), (0,)), ((), ()))
NT = (((1,), (1,)), ((), ()))
TN = (((0,), (0,)), ((), ()))


def dot(a, b, dims=NN):
    return lax.dot_general(a, b, dims, preferred_element_type=F32)


def iota(shape, axis, dtype=jnp.int32):
    return lax.broadcasted_iota(dtype, shape, axis)


def ones_where(mask):
    return jnp.where(mask, 1.0, 0.0).astype(BF16)


def index_kernel(owners, own_rows, rows_ref, lens_ref, w_ref, code_ref, ct_ref, own_hot, row_hot):
    tables, slots, samples = rows_ref.shape
    shift = own_rows.bit_length() - 1
    pieces = own_rows // LANES
    before = ones_where(iota((own_rows, own_rows), 0) < iota((own_rows, own_rows), 1))
    owner_ids = iota((owners, samples), 0)
    row_ids = iota((own_rows, samples), 0)
    chunk = 256
    chunk_ids = iota((chunk, samples), 0)
    for t in range(tables):
        rows = rows_ref[t]
        own = rows >> shift
        loc = rows & (own_rows - 1)
        usable = iota((slots, samples), 0) < lens_ref[t : t + 1, :]
        mass = jnp.where(usable, w_ref[t].astype(F32), 0.0)
        own_used = jnp.where(usable, own, -1)
        for l in range(slots):
            cols = slice(l * samples, (l + 1) * samples)
            own_hot[:, cols] = ones_where(owner_ids == own_used[l : l + 1, :])
            row_hot[:, cols] = ones_where(row_ids == loc[l : l + 1, :])
        present = dot(own_hot[...], row_hot[...], NT) > 0.0
        rank = dot(ones_where(present), before)
        code = jnp.where(present, rank, -1.0)
        for c in range(pieces):
            code_ref[:, t * pieces + c, :] = code[:, c * LANES : (c + 1) * LANES]
        look = dot(rank.astype(BF16), row_hot[...])
        spots = []
        for l in range(slots):
            cols = slice(l * samples, (l + 1) * samples)
            found = jnp.where(owner_ids == own_used[l : l + 1, :], look[:, cols], 0.0)
            rank_l = jnp.sum(found, axis=0, keepdims=True).astype(jnp.int32)
            spots.append(own[l : l + 1, :] * CAP + rank_l)

        def fill(step, _, t=t, spots=spots, mass=mass):
            base = pl.multiple_of(step * chunk, chunk)
            acc = jnp.zeros((chunk, samples), F32)
            for l in range(slots):
                acc = acc + jnp.where(chunk_ids == spots[l] - base, mass[l : l + 1, :], 0.0)
            ct_ref[t, pl.ds(base, chunk), :] = acc.astype(BF16)
            return 0

        lax.fori_loop(0, owners * CAP // chunk, fill, 0)


def fill_hot(code_ref, hot, t, first, count, pieces):
    rank_ids = iota((CAP, LANES), 0).astype(F32)
    for d in range(count):
        codes = code_ref[first + d].astype(F32)
        for c in range(pieces):
            at = t * pieces + c
            hot[d * CAP : (d + 1) * CAP, c * LANES : (c + 1) * LANES] = ones_where(
                rank_ids == codes[at : at + 1, :]
            )


def fetch_kernel(tables, code_ref, emb_ref, out_ref, low, hot):
    devices = code_ref.shape[0]
    pieces = code_ref.shape[1] // tables
    own_rows = low.shape[1]
    halves = low.shape[2] // LANES
    for t in range(tables):
        for h in range(halves):
            at = h * tables + t
            low[t, :, h * LANES : (h + 1) * LANES] = emb_ref[
                pl.ds(at, own_rows, stride=tables * halves), :
            ].astype(BF16)
    group = hot.shape[0] // CAP

    def body(step, _):
        first = step * group
        for t in range(tables):
            fill_hot(code_ref, hot, t, first, group, pieces)
            got = dot(hot[...], low[t]).astype(BF16)
            out_ref[pl.ds(first, group), t * CAP : (t + 1) * CAP, :] = got.reshape(group, CAP, -1)
        return 0

    lax.fori_loop(0, devices // group, body, 0)


def dense_kernel(
    ct_ref, got_ref, dense_ref, labels_ref, head_ref, cross_hbm, hidden_hbm, out_ref,
    cross, hidden_w, joined, before, sems,
):
    tables, spots, samples = ct_ref.shape
    owners = spots // CAP
    width = dense_ref.shape[1]
    copy_cross = pltpu.make_async_copy(cross_hbm, cross, sems.at[0])
    copy_hidden = pltpu.make_async_copy(hidden_hbm, hidden_w, sems.at[1])
    copy_cross.start()
    copy_hidden.start()
    joined[:, :width] = dense_ref[...]
    for t in range(tables):
        got = got_ref[:, t * CAP : (t + 1) * CAP, :].reshape(spots, width)
        joined[:, (t + 1) * width : (t + 2) * width] = dot(ct_ref[t], got, TN).astype(BF16)
    copy_cross.wait()
    widened = joined[...].astype(F32)
    crossed = dot(joined[...], cross[...])
    layered = (widened * crossed + widened).astype(BF16)
    copy_hidden.wait()
    units = hidden_w.shape[1]
    chunk = 512
    logits = jnp.zeros((samples, 1), F32)
    for n in range(units // chunk):
        cols = slice(n * chunk, (n + 1) * chunk)
        part = dot(layered, hidden_w[:, cols])
        before[:, cols] = part
        active = jnp.maximum(part, 0.0).astype(BF16).astype(F32)
        logits = logits + jnp.sum(active * head_ref[:, cols], axis=1, keepdims=True)
    diagonal = iota((samples, samples), 0) == iota((samples, samples), 1)
    marks = jnp.sum(
        jnp.where(diagonal, labels_ref[...].astype(F32), 0.0), axis=1, keepdims=True
    )
    slope = (jax.nn.sigmoid(logits) - marks) * loss_scale
    back = jnp.zeros((samples, layered.shape[1]), F32)
    for n in range(units // chunk):
        cols = slice(n * chunk, (n + 1) * chunk)
        grad = jnp.where(before[:, cols] > 0.0, slope * head_ref[:, cols], 0.0).astype(BF16)
        back = back + dot(grad, hidden_w[:, cols], NT)
    mixed = (back * widened).astype(BF16)
    for t in range(tables):
        cols = slice((t + 1) * width, (t + 2) * width)
        total = back[:, cols] * (crossed[:, cols] + 1.0) + dot(mixed, cross[cols, :], NT)
        grads = total.astype(BF16)
        share = dot(ct_ref[t], grads).astype(BF16)
        out_ref[:, t * CAP : (t + 1) * CAP, :] = share.reshape(owners, CAP, width)


def collect_kernel(tables, code_ref, share_ref, out_ref, hot):
    devices = code_ref.shape[0]
    pieces = code_ref.shape[1] // tables
    own_rows = out_ref.shape[1]
    width = out_ref.shape[2]
    top = code_ref[0].astype(F32)
    for d in range(1, devices):
        top = jnp.maximum(top, code_ref[d].astype(F32))
    top = jnp.transpose(top)
    for t in range(tables):
        fill_hot(code_ref, hot, t, 0, devices, pieces)
        shares = share_ref[:, t * CAP : (t + 1) * CAP, :].reshape(devices * CAP, width)
        for c in range(pieces):
            grad = dot(hot[:, c * LANES : (c + 1) * LANES], shares, TN)
            at = t * pieces + c
            out_ref[t, c * LANES : (c + 1) * LANES, :] = jnp.where(
                top[:, at : at + 1] >= 0.0, grad, UNTOUCHED
            )


def adam_kernel(mine_ref, peer_ref, first_ref, second_ref, first_out, second_out, step_out, tall):
    tables, own_rows, width = mine_ref.shape
    pieces = own_rows // LANES
    halves = width // LANES
    for t in range(tables):
        for c in range(pieces):
            tall[t * pieces + c : t * pieces + c + 1, :] = second_ref[
                t : t + 1, c * LANES : (c + 1) * LANES
            ]
    second_all = jnp.transpose(tall[...])
    for t in range(tables):
        for c in range(pieces):
            at = t * pieces + c
            rows = slice(c * LANES, (c + 1) * LANES)
            second = second_all[:, at : at + 1]
            begin = c * LANES * tables * halves
            views = [
                pl.ds(begin + h * tables + t, LANES, stride=tables * halves) for h in range(halves)
            ]
            first = jnp.concatenate([first_ref[v, :] for v in views], axis=1)
            first_sum = 0.0
            second_sum = 0.0
            step_sum = 0.0
            for ref in (mine_ref, peer_ref):
                grad = ref[t, rows, :]
                touched = grad < UNTOUCHED
                touched_row = touched[:, :1]
                grown = beta_second * second + (1.0 - beta_second) * jnp.mean(
                    grad * grad, axis=1, keepdims=True
                )
                second_new = jnp.where(grad[:, :1] < UNTOUCHED, grown, second)
                first_new = jnp.where(
                    touched, beta_first * first + (1.0 - beta_first) * grad, first
                )
                step = jnp.where(touched, first_new / (jnp.sqrt(second_new) + epsilon), 0.0)
                first_sum = first_sum + first_new
                second_sum = second_sum + second_new
                step_sum = step_sum + step
            first_sum = first_sum * 0.5
            step_sum = step_sum * 0.5
            for h, v in enumerate(views):
                first_out[v, :] = first_sum[:, h * LANES : (h + 1) * LANES]
                step_out[v, :] = step_sum[:, h * LANES : (h + 1) * LANES]
            tall[at : at + 1, :] = jnp.transpose(
                jnp.broadcast_to(second_sum * 0.5, (LANES, LANES))
            )[:1, :]
    for t in range(tables):
        for c in range(pieces):
            at = t * pieces + c
            second_out[t : t + 1, c * LANES : (c + 1) * LANES] = tall[at : at + 1, :]


def to_rows(x):
    rows, tables, width = x.shape
    split = x.reshape(rows, tables, width // LANES, LANES)
    return jnp.transpose(split, (0, 2, 1, 3)).reshape(-1, LANES)


def from_rows(x, rows, tables, width):
    split = x.reshape(rows, width // LANES, tables, LANES)
    return jnp.transpose(split, (0, 2, 1, 3)).reshape(rows, tables, width)


def call(body, out_shape, scratch, *operands, in_hbm=()):
    vmem = pl.BlockSpec(memory_space=pltpu.VMEM)
    hbm = pl.BlockSpec(memory_space=pl.ANY)
    single = not isinstance(out_shape, tuple)
    return pl.pallas_call(
        body,
        out_shape=out_shape,
        in_specs=[hbm if n in in_hbm else vmem for n in range(len(operands))],
        out_specs=vmem if single else tuple(vmem for _ in out_shape),
        scratch_shapes=scratch,
        compiler_params=pltpu.CompilerParams(vmem_limit_bytes=VMEM_LIMIT),
    )(*operands)


def local(
    owners,
    replicas,
    dense_input,
    bag_rows,
    bag_lengths,
    bag_weights,
    labels,
    embedding,
    first_moment,
    second_moment,
    cross_weight,
    hidden_weight,
    head_weight,
):
    samples, tables, slots = bag_rows.shape
    own_rows, _, width = embedding.shape
    pieces = own_rows // LANES
    shape = jax.ShapeDtypeStruct
    code, ct = call(
        functools.partial(index_kernel, owners, own_rows),
        (
            shape((owners, tables * pieces, LANES), F32),
            shape((tables, owners * CAP, samples), BF16),
        ),
        [
            pltpu.VMEM((owners, slots * samples), BF16),
            pltpu.VMEM((own_rows, slots * samples), BF16),
        ],
        jnp.transpose(bag_rows, (1, 2, 0)),
        jnp.transpose(bag_lengths),
        jnp.transpose(bag_weights, (1, 2, 0)),
    )
    asked = lax.all_to_all(code.astype(BF16), "shard", 0, 0, tiled=True)
    found = call(
        functools.partial(fetch_kernel, tables),
        shape((owners, tables * CAP, width), BF16),
        [
            pltpu.VMEM((tables, own_rows, width), BF16),
            pltpu.VMEM((8 * CAP, own_rows), BF16),
        ],
        asked,
        to_rows(embedding),
    )
    got = lax.all_to_all(found, "shard", 0, 0, tiled=True)
    share = call(
        dense_kernel,
        shape((owners, tables * CAP, width), BF16),
        [
            pltpu.VMEM(cross_weight.shape, BF16),
            pltpu.VMEM(hidden_weight.shape, BF16),
            pltpu.VMEM((samples, cross_weight.shape[0]), BF16),
            pltpu.VMEM((samples, hidden_weight.shape[1]), F32),
            pltpu.SemaphoreType.DMA((2,)),
        ],
        ct,
        got,
        dense_input,
        labels.reshape(1, samples),
        head_weight.astype(F32).reshape(1, -1),
        cross_weight,
        hidden_weight,
        in_hbm=(5, 6),
    )
    shares = lax.all_to_all(share, "shard", 0, 0, tiled=True)
    mine = call(
        functools.partial(collect_kernel, tables),
        shape((tables, own_rows, width), F32),
        [pltpu.VMEM((owners * CAP, own_rows), BF16)],
        asked,
        shares,
    )
    peer = lax.ppermute(mine, "replica", [(0, 1), (1, 0)])
    first, second, step = call(
        adam_kernel,
        (
            shape((own_rows * tables * width // LANES, LANES), F32),
            shape((tables, own_rows), F32),
            shape((own_rows * tables * width // LANES, LANES), F32),
        ),
        [pltpu.VMEM((tables * pieces, LANES), F32)],
        mine,
        peer,
        to_rows(first_moment),
        jnp.transpose(second_moment),
    )
    return (
        from_rows(first, own_rows, tables, width),
        jnp.transpose(second),
        from_rows(step, own_rows, tables, width),
    )


def solution(mesh):
    placed = (
        P(("replica", "shard"), None),
        P(("replica", "shard"), None, None),
        P(("replica", "shard"), None),
        P(("replica", "shard"), None, None),
        P(("replica", "shard")),
        P("shard", None, None),
        P("shard", None, None),
        P("shard", None),
        P(),
        P(),
        P(),
    )
    return jax.shard_map(
        functools.partial(local, mesh.shape["shard"], mesh.shape["replica"]),
        mesh=mesh,
        in_specs=placed,
        out_specs=(P("shard", None, None), P("shard", None), P("shard", None, None)),
        check_vma=False,
    )
```

time: 828 us -> 135 us (0.16)
  waiting for transfers between devices: 525 us -> 29.4 us
  blocking collectives: 157 us -> 54.9 us
  other arithmetic: 86.9 us -> 1.57 us
  Pallas kernels: 0 us -> 37 us
  matrix products: 34 us -> 0 us
  between operations: 14.1 us -> 0.67 us
    reduce_scatter x1 -> x0, waiting for transfers between devices: 361 us -> none  [local(): lax.psum_scatter(jnp.einsum('gtr,rte->gte', block, embedding_low, preferr...]
    all_gather x1 -> x0, blocking collectives: 154 us -> none  [local(): lax.all_gather(masked_low, 'shard', axis=0, tiled=True)]
    all_gather x2 -> x0, waiting for transfers between devices: 140 us -> none  [the longest x1 140 us: local(): lax.all_gather(bag_grads, 'shard', axis=0, tiled=True)]
    reduce_sum x1 -> x0, other arithmetic: 76.3 us -> none  [local(): hits = jnp.transpose(jnp.sum(group_counts, axis=0))]
    all_to_all x0 -> x2, blocking collectives: none -> 54.9 us  [the longest x1 34.3 us: local(): shares = lax.all_to_all(share, 'shard', 0, 0, tiled=True)]
    pallas_call x0 -> x5, Pallas kernels: none -> 37 us  [call(): pl.pallas_call(body, out_shape=out_shape, in_specs=[hbm if n in in_hbm el...]
    dot_general x7 -> x0, matrix products: 34 us -> none  [the longest x1 16 us: local(): jnp.einsum('gtr,rte->gte', block, embedding_low, preferred_element_type=j...]
    all_to_all x0 -> x1, waiting for transfers between devices: none -> 26.9 us  [local(): got = lax.all_to_all(found, 'shard', 0, 0, tiled=True)]
  transfers between devices with their start and end apart: 4 -> 2, of which waited for: 3 -> 2; matrix products, arithmetic and copies ran while one was open for 1% -> 0% of each run, Pallas kernels for 0% -> 0%
where the time goes in v1:
time: 135 us; the launch traced here: 134 us
  blocking collectives  54.9 us (41%)
  Pallas kernels  37 us (27%)
  waiting for transfers between devices  29.4 us (22%)
  starting transfers between devices  8.38 us (6%)
  local copies, waits for them, and re-layouts  2.32 us (2%)
  other arithmetic  1.57 us (1%)
    pallas_call x5, Pallas kernels, call(): pl.pallas_call(body, out_shape=out_shape, in_specs=[hbm if n in in_hbm el...  37 us
    all_to_all x1, blocking collectives, local(): shares = lax.all_to_all(share, 'shard', 0, 0, tiled=True)  34.3 us
    all_to_all x1, waiting for transfers between devices, local(): got = lax.all_to_all(found, 'shard', 0, 0, tiled=True)  26.9 us
    all_to_all x1, blocking collectives, local(): asked = lax.all_to_all(code.astype(BF16), 'shard', 0, 0, tiled=True)  20.6 us
    all_to_all x1, starting transfers between devices, local(): got = lax.all_to_all(found, 'shard', 0, 0, tiled=True)  5.07 us
    ppermute x1, starting transfers between devices, local(): peer = lax.ppermute(mine, 'replica', [(0, 1), (1, 0)])  3.31 us
  transfers between devices with their start and end apart: 2, of which 2 were waited for; matrix products, arithmetic and copies ran while one was open for 0% of the time, Pallas kernels for 0%

profile of v1, /device:TPU:1, one launch (start us, length us, event | category | flops | bytes accessed | tf_op | source)
XLA Modules:
  0.0 134.3 jit_solution(17082799287804057260)
XLA Ops:
  0.6 9.6 %shard_map.130 = (f32[64,8,128]{2,1,0:T(8,128)}, bf16[2,2048,128]{2,1,0:T(8,128)(2,1)}) custom-call(s32[2,16,128]{2,1,0:T(8,128)} %bitcast.30, s32[2,128]{1,0:T(2,128)} %bitcast.33, bf16[2,16,128]{2,1,0:T(8,128)(2,1)} %bitcast.31), custom_call_target="tpu_custom_call" | custom-call | tf_op jit(solution)/shard_map/pallas_call | solution.py:253
  10.2 1.0 convert_element_type.4
  11.2 20.6 %all_to_all.15.code_ref = bf16[64,8,128]{2,1,0:T(8,128)(2,1)} all-to-all(bf16[64,8,128]{2,1,0:T(8,128)(2,1)S(1)} %convert_element_type.4), channel_id=1, replica_groups=mesh['replica'=2,'shard'=64] {'shard'}, dimensions={0} | all-to-all | bytes 262144 | tf_op jit(solution)/shard_map/all_to_all | solution.py:296
  31.8 5.4 %shard_map.131 = bf16[64,64,256]{2,1,0:T(8,128)(2,1)} custom-call(bf16[64,8,128]{2,1,0:T(8,128)(2,1)} %all_to_all.15.code_ref, f32[2048,128]{1,0:T(8,128)} %bitcast.27), custom_call_target="tpu_custom_call" | custom-call | tf_op jit(solution)/shard_map/pallas_call | solution.py:253
  37.3 0.0 copy-start.2
  37.3 5.1 %all-to-all-start.1 = ((bf16[64,64,256]{2,1,0:T(8,128)(2,1)}), bf16[64,64,256]{2,1,0:T(8,128)(2,1)S(1)}, u32[]{:S(2)}, u32[]{:S(2)}) async-start(bf16[64,64,256]{2,1,0:T(8,128)(2,1)} %shard_map.131), calls=%async_computation.1 | async-start | bytes 4194304 | tf_op jit(solution)/shard_map/all_to_all | solution.py:307
  42.4 0.0 copy-done.2
  42.4 0.6 reshape.49
  43.0 26.9 %all-to-all-done.1.got_ref = bf16[64,64,256]{2,1,0:T(8,128)(2,1)S(1)} async-done(((bf16[64,64,256]{2,1,0:T(8,128)(2,1)}), bf16[64,64,256]{2,1,0:T(8,128)(2,1)S(1)}, u32[]{:S(2)}, u32[]{:S(2)}) %all-to-all-start.1) | async-done | bytes 2097184 | tf_op jit(solution)/shard_map/all_to_all | solution.py:307
  69.9 0.0 copy-start
  69.9 1.3 %copy-done = bf16[64,64,256]{2,1,0:T(8,128)(2,1)} copy-done((bf16[64,64,256]{2,1,0:T(8,128)(2,1)}, bf16[64,64,256]{2,1,0:T(8,128)(2,1)S(1)}, u32[]{:S(2)}) %copy-start) | copy-done | bytes 2097176
  71.3 11.4 %shard_map.132 = bf16[64,64,256]{2,1,0:T(8,128)(2,1)} custom-call(bf16[2,2048,128]{2,1,0:T(8,128)(2,1)} %get-tuple-element.9.ct_ref, bf16[64,64,256]{2,1,0:T(8,128)(2,1)} %copy-done, bf16[128,256]{1,0:T(8,128)(2,1)} %dense_ref.1, s32[1,128]{1,0:T(1,128)} %bitcast.34, f32[1,4096]{1,0:T(1,128)} %bitcast.29, bf16[768,768]{1,0:T(8,128)(2,1)} %cross_hbm.1, ...), custom_call_target="tpu_custom_call" | custom-call | tf_op jit(solution)/shard_map/pallas_call | solution.py:253
  82.7 34.3 %all_to_all.16.share_ref = bf16[64,64,256]{2,1,0:T(8,128)(2,1)} all-to-all(bf16[64,64,256]{2,1,0:T(8,128)(2,1)} %shard_map.132), channel_id=1, replica_groups=mesh['replica'=2,'shard'=64] {'shard'}, dimensions={0} | all-to-all | bytes 4194304 | tf_op jit(solution)/shard_map/all_to_all | solution.py:327
  116.9 4.9 %shard_map.133.mine_ref = f32[2,512,256]{2,1,0:T(8,128)} custom-call(bf16[64,8,128]{2,1,0:T(8,128)(2,1)} %all_to_all.15.code_ref, bf16[64,64,256]{2,1,0:T(8,128)(2,1)} %all_to_all.16.share_ref), custom_call_target="tpu_custom_call" | custom-call | tf_op jit(solution)/shard_map/pallas_call | solution.py:253
  121.8 3.3 %collective-permute-start = (f32[2,512,256]{2,1,0:T(8,128)}, f32[2,512,256]{2,1,0:T(8,128)S(1)}, u32[]{:S(2)}, u32[]{:S(2)}) collective-permute-start(f32[2,512,256]{2,1,0:T(8,128)} %shard_map.133.mine_ref), channel_id=1, source_target_pairs={{0,64},{64,0},{1,65},{65,1},{2,66},{66,2},{3,67},{67,3},{4,68},{68... | collective-permute-start | bytes 3145736 | tf_op jit(solution)/shard_map/ppermute | solution.py:335
  125.1 2.5 %collective-permute-done.peer_ref = f32[2,512,256]{2,1,0:T(8,128)S(1)} collective-permute-done((f32[2,512,256]{2,1,0:T(8,128)}, f32[2,512,256]{2,1,0:T(8,128)S(1)}, u32[]{:S(2)}, u32[]{:S(2)}) %collective-permute-start) | collective-permute-done | bytes 1048608 | tf_op jit(solution)/shard_map/ppermute | solution.py:335
  127.6 0.0 copy-start.1
  127.6 1.0 copy-done.1
  128.6 5.7 %shard_map.134 = (f32[2048,128]{1,0:T(8,128)}, f32[2,512]{1,0:T(2,128)}, f32[2048,128]{1,0:T(8,128)}) custom-call(f32[2,512,256]{2,1,0:T(8,128)} %shard_map.133.mine_ref, f32[2,512,256]{2,1,0:T(8,128)} %copy-done.1, f32[2048,128]{1,0:T(8,128)} %bitcast.28, f32[2,512]{1,0:T(2,128)} %bitcast.32), custom_call_target="tpu_custom_call" | custom-call | tf_op jit(solution)/shard_map/pallas_call | solution.py:253
Async XLA Ops:
  37.3 5.1 %copy-start.2 = (bf16[4096]{0:T(1024)(128)(2,1)S(1)}, bf16[4096]{0:T(1024)(128)(2,1)}, u32[]{:S(2)}) copy-start(bf16[4096]{0:T(1024)(128)(2,1)} %param.21) | copy-start | bytes 24580
  37.3 32.6 %all-to-all-start.1 = ((bf16[64,64,256]{2,1,0:T(8,128)(2,1)}), bf16[64,64,256]{2,1,0:T(8,128)(2,1)S(1)}, u32[]{:S(2)}, u32[]{:S(2)}) async-start(bf16[64,64,256]{2,1,0:T(8,128)(2,1)} %shard_map.131), calls=%async_computation.1 | async-start | bytes 4194304 | tf_op jit(solution)/shard_map/all_to_all | solution.py:307
  69.9 1.3 %copy-start = (bf16[64,64,256]{2,1,0:T(8,128)(2,1)}, bf16[64,64,256]{2,1,0:T(8,128)(2,1)S(1)}, u32[]{:S(2)}) copy-start(bf16[64,64,256]{2,1,0:T(8,128)(2,1)S(1)} %all-to-all-done.1.got_ref) | copy-start | bytes 6291460
  121.8 5.8 %collective-permute-start = (f32[2,512,256]{2,1,0:T(8,128)}, f32[2,512,256]{2,1,0:T(8,128)S(1)}, u32[]{:S(2)}, u32[]{:S(2)}) collective-permute-start(f32[2,512,256]{2,1,0:T(8,128)} %shard_map.133.mine_ref), channel_id=1, source_target_pairs={{0,64},{64,0},{1,65},{65,1},{2,66},{66,2},{3,67},{67,3},{4,68},{68... | collective-permute-start | bytes 3145736 | tf_op jit(solution)/shard_map/ppermute | solution.py:335
  127.6 1.0 copy-start.1

commit v2 on v1

v2 whole, which is shorter than its diff:
```python
import functools

import jax
import jax.numpy as jnp
from jax import lax
from jax.experimental import pallas as pl
from jax.experimental.pallas import tpu as pltpu
from jax.sharding import PartitionSpec as P

loss_scale = 64.0
beta_first = 0.9
beta_second = 0.99
epsilon = 1e-08

CAP = 32
LANES = 128
GROUP = 8
F32 = jnp.float32
BF16 = jnp.bfloat16
HOT = jnp.float8_e4m3fn
MIB = 1024 * 1024

NN = (((1,), (0,)), ((), ()))
NT = (((1,), (1,)), ((), ()))
TN = (((0,), (0,)), ((), ()))


def dot(a, b, dims=NN):
    return lax.dot_general(a, b, dims, preferred_element_type=F32)


def iota(shape, axis, dtype=jnp.int32):
    return lax.broadcasted_iota(dtype, shape, axis)


def ones_where(mask):
    return jnp.where(mask, 1.0, 0.0).astype(BF16)


def matches(ids, row):
    wanted = jnp.broadcast_to(row, ids.shape).astype(BF16)
    return jnp.where(ids == wanted, jnp.ones_like(ids), jnp.zeros_like(ids))


def fill_row_hot(row_hot, l, row):
    own_rows = row_hot.shape[0]
    samples = row.shape[1]
    block = 256
    ids = iota((block, samples), 0).astype(F32).astype(BF16)
    for n in range(own_rows // block):
        inside = row - n * block
        inside = jnp.where((inside >= 0.0) & (inside < block), inside, -1.0)
        row_hot[n * block : (n + 1) * block, l * samples : (l + 1) * samples] = matches(ids, inside)


def index_kernel(owners, own_rows, rows_ref, lens_ref, code_ref, rank_ref, own_hot, row_hot, wide):
    tables, slots, samples = rows_ref.shape
    shift = own_rows.bit_length() - 1
    pieces = own_rows // LANES
    before = ones_where(iota((own_rows, own_rows), 0) < iota((own_rows, own_rows), 1))
    owner_ids = iota((owners, samples), 0)
    for t in range(tables):
        rows = rows_ref[t]
        usable = iota((slots, samples), 0) < lens_ref[t : t + 1, :]
        own = jnp.where(usable, rows >> shift, -1)
        loc = (rows & (own_rows - 1)).astype(F32)
        for l in range(slots):
            cols = slice(l * samples, (l + 1) * samples)
            own_hot[:, cols] = ones_where(owner_ids == own[l : l + 1, :])
            fill_row_hot(row_hot, l, loc[l : l + 1, :])
        present = dot(own_hot[...], row_hot[...], NT) > 0.0
        rank = dot(ones_where(present), before)
        code = jnp.where(present, rank, -1.0)
        for c in range(pieces):
            wide[:, t * pieces + c, :] = code[:, c * LANES : (c + 1) * LANES]
        rank_ref[t] = rank.astype(BF16)
    code_ref[...] = wide[...].astype(BF16)


def weigh_kernel(rows_ref, lens_ref, w_ref, rank_ref, ct_ref, row_hot):
    tables, slots, samples = rows_ref.shape
    owners, own_rows = rank_ref.shape[1:]
    shift = own_rows.bit_length() - 1
    owner_ids = iota((owners, samples), 0)
    chunk = 256
    chunk_ids = iota((chunk, samples), 0)
    for t in range(tables):
        rows = rows_ref[t]
        own = rows >> shift
        loc = (rows & (own_rows - 1)).astype(F32)
        usable = iota((slots, samples), 0) < lens_ref[t : t + 1, :]
        mass = jnp.where(usable, w_ref[t].astype(F32), 0.0)
        for l in range(slots):
            fill_row_hot(row_hot, l, loc[l : l + 1, :])
        look = dot(rank_ref[t], row_hot[...])
        spots = []
        for l in range(slots):
            cols = slice(l * samples, (l + 1) * samples)
            found = jnp.where(owner_ids == own[l : l + 1, :], look[:, cols], 0.0)
            rank_l = jnp.sum(found, axis=0, keepdims=True).astype(jnp.int32)
            spots.append(own[l : l + 1, :] * CAP + rank_l)

        def fill(step, _, t=t, spots=spots, mass=mass):
            base = pl.multiple_of(step * chunk, chunk)
            acc = jnp.zeros((chunk, samples), F32)
            for l in range(slots):
                acc = acc + jnp.where(chunk_ids == spots[l] - base, mass[l : l + 1, :], 0.0)
            ct_ref[t, pl.ds(base, chunk), :] = acc.astype(BF16)
            return 0

        lax.fori_loop(0, owners * CAP // chunk, fill, 0)


def hot_rows(codes, rank_ids, t, pieces):
    return [
        matches(rank_ids, codes[t * pieces + c : t * pieces + c + 1, :])
        for c in range(pieces)
    ]


def low_kernel(tables, emb_ref, low_ref):
    own_rows, width = low_ref.shape[1:]
    halves = width // LANES
    for t in range(tables):
        for h in range(halves):
            view = pl.ds(h * tables + t, own_rows, stride=tables * halves)
            low_ref[t, :, h * LANES : (h + 1) * LANES] = emb_ref[view, :].astype(BF16)


def fetch_kernel(code_ref, low_ref, out_hbm, hot, out, sems):
    devices = code_ref.shape[0]
    tables = low_ref.shape[0]
    pieces = code_ref.shape[1] // tables
    group = hot.shape[1] // CAP
    rank_ids = iota((CAP, LANES), 0).astype(F32).astype(BF16)

    def body(step, _):
        first = step * group
        for d in range(group):
            codes = code_ref[first + d].astype(F32)
            for t in range(tables):
                for c, part in enumerate(hot_rows(codes, rank_ids, t, pieces)):
                    hot[t, d * CAP : (d + 1) * CAP, c * LANES : (c + 1) * LANES] = part
        for t in range(tables):
            got = dot(hot[t], low_ref[t]).astype(BF16)
            out[pl.ds(first, group), t * CAP : (t + 1) * CAP, :] = got.reshape(group, CAP, -1)
        send(step).start()
        return 0

    def send(step):
        block = pl.ds(step * group, group)
        return pltpu.make_async_copy(out.at[block], out_hbm.at[block], sems.at[step])

    steps = devices // group
    lax.fori_loop(0, steps, body, 0)
    for step in range(steps):
        send(step).wait()


def dense_kernel(
    ct_ref, got_ref, dense_ref, labels_ref, head_ref, cross_hbm, hidden_hbm, out_hbm,
    cross, hidden_w, joined, before, out, sems, out_sems,
):
    tables, spots, samples = ct_ref.shape
    owners = spots // CAP
    width = dense_ref.shape[1]
    copy_cross = pltpu.make_async_copy(cross_hbm, cross, sems.at[0])
    copy_hidden = pltpu.make_async_copy(hidden_hbm, hidden_w, sems.at[1])
    copy_cross.start()
    copy_hidden.start()
    joined[:, :width] = dense_ref[...]
    for t in range(tables):
        got = got_ref[:, t * CAP : (t + 1) * CAP, :].reshape(spots, width)
        joined[:, (t + 1) * width : (t + 2) * width] = dot(ct_ref[t], got, TN).astype(BF16)
    copy_cross.wait()
    widened = joined[...].astype(F32)
    crossed = dot(joined[...], cross[...])
    layered = (widened * crossed + widened).astype(BF16)
    copy_hidden.wait()
    units = hidden_w.shape[1]
    chunk = 512
    logits = jnp.zeros((samples, 1), F32)
    for n in range(units // chunk):
        cols = slice(n * chunk, (n + 1) * chunk)
        part = dot(layered, hidden_w[:, cols])
        before[:, cols] = part
        active = jnp.maximum(part, 0.0).astype(BF16).astype(F32)
        logits = logits + jnp.sum(active * head_ref[:, cols], axis=1, keepdims=True)
    diagonal = iota((samples, samples), 0) == iota((samples, samples), 1)
    marks = jnp.sum(
        jnp.where(diagonal, labels_ref[...].astype(F32), 0.0), axis=1, keepdims=True
    )
    slope = (jax.nn.sigmoid(logits) - marks) * loss_scale
    back = jnp.zeros((samples, layered.shape[1]), F32)
    for n in range(units // chunk):
        cols = slice(n * chunk, (n + 1) * chunk)
        grad = jnp.where(before[:, cols] > 0.0, slope * head_ref[:, cols], 0.0).astype(BF16)
        back = back + dot(grad, hidden_w[:, cols], NT)
    mixed = (back * widened).astype(BF16)
    steps = out_sems.shape[0]
    part_rows = spots // steps
    part_owners = owners // steps

    def send(n):
        block = pl.ds(n * part_owners, part_owners)
        return pltpu.make_async_copy(out.at[block], out_hbm.at[block], out_sems.at[n])

    for t in range(tables):
        cols = slice((t + 1) * width, (t + 2) * width)
        total = back[:, cols] * (crossed[:, cols] + 1.0) + dot(mixed, cross[cols, :], NT)
        grads = total.astype(BF16)
        for n in range(steps):
            share = dot(ct_ref[t, n * part_rows : (n + 1) * part_rows, :], grads).astype(BF16)
            block = slice(n * part_owners, (n + 1) * part_owners)
            out[block, t * CAP : (t + 1) * CAP, :] = share.reshape(part_owners, CAP, width)
            if t == tables - 1:
                send(n).start()
    for n in range(steps):
        send(n).wait()


def spread_kernel(tables, code_ref, second_ref, hot_ref, columns_ref, tall):
    devices = code_ref.shape[0]
    pieces = code_ref.shape[1] // tables
    count = tables * pieces
    rank_ids = iota((CAP, LANES), 0).astype(F32).astype(BF16)
    group = LANES // CAP

    def body(step, top):
        first = step * group
        codes = [code_ref[first + d].astype(F32) for d in range(group)]
        for t in range(tables):
            parts = [hot_rows(code, rank_ids, t, pieces) for code in codes]
            for c in range(pieces):
                block = jnp.concatenate([part[c] for part in parts], axis=0)
                hot_ref[
                    t, c * LANES : (c + 1) * LANES, pl.ds(pl.multiple_of(step * LANES, LANES), LANES)
                ] = jnp.transpose(block).astype(HOT)
        for code in codes:
            top = jnp.maximum(top, code)
        return top

    top = lax.fori_loop(0, devices // group, body, jnp.full((count, LANES), -1.0, F32))
    tall[...] = jnp.zeros_like(tall)
    tall[:count, :] = top
    for t in range(tables):
        for c in range(pieces):
            at = count + t * pieces + c
            tall[at : at + 1, :] = second_ref[t : t + 1, c * LANES : (c + 1) * LANES]
    columns_ref[...] = jnp.transpose(tall[...])


def collect_kernel(hot_ref, columns_ref, share_ref, out_ref):
    tables, own_rows, spots = hot_ref.shape
    width = share_ref.shape[2]
    pieces = own_rows // LANES
    count = tables * pieces
    lane_ids = iota((LANES, LANES), 1)
    stats = jnp.zeros((LANES, LANES), F32)
    for t in range(tables):
        shares = share_ref[:, t * CAP : (t + 1) * CAP, :].reshape(spots, width)
        for c in range(pieces):
            at = t * pieces + c
            grad = dot(hot_ref[t, c * LANES : (c + 1) * LANES, :].astype(BF16), shares)
            touched = columns_ref[:, at : at + 1] >= 0.0
            second = columns_ref[:, count + at : count + at + 1]
            mean = jnp.mean(grad * grad, axis=1, keepdims=True)
            second = jnp.where(
                touched, beta_second * second + (1.0 - beta_second) * mean, second
            )
            scale = jnp.where(touched, 1.0 / (jnp.sqrt(second) + epsilon), 0.0)
            decay = jnp.where(touched, beta_first, 1.0)
            stats = jnp.where(lane_ids == at, second, stats)
            stats = jnp.where(lane_ids == count + at, scale, stats)
            stats = jnp.where(lane_ids == 2 * count + at, decay, stats)
            out_ref[at * LANES : (at + 1) * LANES, :] = (1.0 - beta_first) * grad
    out_ref[count * LANES :, :LANES] = stats
    out_ref[count * LANES :, LANES:] = jnp.zeros((LANES, width - LANES), F32)


def adam_kernel(mine_ref, peer_ref, first_ref, first_out, second_out, step_out):
    tables, own_rows = second_out.shape
    width = mine_ref.shape[1]
    pieces = own_rows // LANES
    halves = width // LANES
    count = tables * pieces
    mine = mine_ref[count * LANES :, :LANES]
    peer = peer_ref[count * LANES :, :LANES]
    second_all = jnp.transpose((mine + peer) * 0.5)
    for t in range(tables):
        for c in range(pieces):
            at = t * pieces + c
            rows = slice(at * LANES, (at + 1) * LANES)
            second_out[t : t + 1, c * LANES : (c + 1) * LANES] = second_all[at : at + 1, :]
            sides = [
                (
                    ref,
                    jnp.broadcast_to(s[:, 2 * count + at : 2 * count + at + 1], (LANES, LANES)),
                    jnp.broadcast_to(s[:, count + at : count + at + 1] * 0.5, (LANES, LANES)),
                )
                for ref, s in ((mine_ref, mine), (peer_ref, peer))
            ]
            for h in range(halves):
                view = pl.ds(
                    c * LANES * count // pieces * halves + h * tables + t,
                    LANES,
                    stride=tables * halves,
                )
                first = first_ref[view, :]
                cols = slice(h * LANES, (h + 1) * LANES)
                firsts = [decay * first + ref[rows, cols] for ref, decay, _ in sides]
                first_out[view, :] = (firsts[0] + firsts[1]) * 0.5
                step_out[view, :] = firsts[0] * sides[0][2] + firsts[1] * sides[1][2]


def to_rows(x):
    rows, tables, width = x.shape
    split = x.reshape(rows, tables, width // LANES, LANES)
    return jnp.transpose(split, (0, 2, 1, 3)).reshape(-1, LANES)


def from_rows(x, rows, tables, width):
    split = x.reshape(rows, width // LANES, tables, LANES)
    return jnp.transpose(split, (0, 2, 1, 3)).reshape(rows, tables, width)


def call(body, mib, out_shape, scratch, *operands, in_hbm=(), out_hbm=False):
    vmem = pl.BlockSpec(memory_space=pltpu.VMEM)
    hbm = pl.BlockSpec(memory_space=pltpu.HBM)
    single = not isinstance(out_shape, tuple)
    return pl.pallas_call(
        body,
        out_shape=out_shape,
        in_specs=[hbm if n in in_hbm else vmem for n in range(len(operands))],
        out_specs=(hbm if out_hbm else vmem) if single else tuple(vmem for _ in out_shape),
        scratch_shapes=scratch,
        compiler_params=pltpu.CompilerParams(vmem_limit_bytes=mib * MIB),
    )(*operands)


def local(
    owners,
    dense_input,
    bag_rows,
    bag_lengths,
    bag_weights,
    labels,
    embedding,
    first_moment,
    second_moment,
    cross_weight,
    hidden_weight,
    head_weight,
):
    samples, tables, slots = bag_rows.shape
    own_rows, _, width = embedding.shape
    pieces = own_rows // LANES
    count = tables * pieces
    spots = owners * CAP
    shape = jax.ShapeDtypeStruct
    rows = jnp.transpose(bag_rows, (1, 2, 0))
    lens = jnp.transpose(bag_lengths)
    code, rank = call(
        functools.partial(index_kernel, owners, own_rows),
        56,
        (
            shape((owners, count, LANES), BF16),
            shape((tables, owners, own_rows), BF16),
        ),
        [
            pltpu.VMEM((owners, slots * samples), BF16),
            pltpu.VMEM((own_rows, slots * samples), BF16),
            pltpu.VMEM((owners, count, LANES), F32),
        ],
        rows,
        lens,
    )
    asked = lax.all_to_all(code, "shard", 0, 0, tiled=True)
    low = call(
        functools.partial(low_kernel, tables),
        6,
        shape((tables, own_rows, width), BF16),
        [],
        to_rows(embedding),
    )
    found = call(
        fetch_kernel,
        50,
        shape((owners, tables * CAP, width), BF16),
        [
            pltpu.VMEM((tables, GROUP * CAP, own_rows), BF16),
            pltpu.VMEM((owners, tables * CAP, width), BF16),
            pltpu.SemaphoreType.DMA((owners // GROUP,)),
        ],
        asked,
        low,
        out_hbm=True,
    )
    got = lax.all_to_all(found, "shard", 0, 0, tiled=True)
    ct = call(
        weigh_kernel,
        12,
        shape((tables, spots, samples), BF16),
        [pltpu.VMEM((own_rows, slots * samples), BF16)],
        rows,
        lens,
        jnp.transpose(bag_weights, (1, 2, 0)),
        rank,
    )
    share = call(
        dense_kernel,
        50,
        shape((owners, tables * CAP, width), BF16),
        [
            pltpu.VMEM(cross_weight.shape, BF16),
            pltpu.VMEM(hidden_weight.shape, BF16),
            pltpu.VMEM((samples, cross_weight.shape[0]), BF16),
            pltpu.VMEM((samples, hidden_weight.shape[1]), F32),
            pltpu.VMEM((owners, tables * CAP, width), BF16),
            pltpu.SemaphoreType.DMA((2,)),
            pltpu.SemaphoreType.DMA((4,)),
        ],
        ct,
        got,
        dense_input,
        labels.reshape(1, samples),
        head_weight.astype(F32).reshape(1, -1),
        cross_weight,
        hidden_weight,
        in_hbm=(5, 6),
        out_hbm=True,
    )
    shares = lax.all_to_all(share, "shard", 0, 0, tiled=True)
    asked_later, _ = lax.optimization_barrier((asked, share))
    hot, columns = call(
        functools.partial(spread_kernel, tables),
        52,
        (shape((tables, own_rows, spots), HOT), shape((LANES, LANES), F32)),
        [pltpu.VMEM((LANES, LANES), F32)],
        asked_later,
        jnp.transpose(second_moment),
    )
    mine = call(
        collect_kernel,
        14,
        shape((count * LANES + LANES, width), F32),
        [],
        hot,
        columns,
        shares,
    )
    peer = lax.ppermute(mine, "replica", [(0, 1), (1, 0)])
    first, second, step = call(
        adam_kernel,
        12,
        (
            shape((own_rows * tables * width // LANES, LANES), F32),
            shape((tables, own_rows), F32),
            shape((own_rows * tables * width // LANES, LANES), F32),
        ),
        [],
        mine,
        peer,
        to_rows(first_moment),
    )
    return (
        from_rows(first, own_rows, tables, width),
        jnp.transpose(second),
        from_rows(step, own_rows, tables, width),
    )


def solution(mesh):
    placed = (
        P(("replica", "shard"), None),
        P(("replica", "shard"), None, None),
        P(("replica", "shard"), None),
        P(("replica", "shard"), None, None),
        P(("replica", "shard")),
        P("shard", None, None),
        P("shard", None, None),
        P("shard", None),
        P(),
        P(),
        P(),
    )
    return jax.shard_map(
        functools.partial(local, mesh.shape["shard"]),
        mesh=mesh,
        in_specs=placed,
        out_specs=(P("shard", None, None), P("shard", None), P("shard", None, None)),
        check_vma=False,
    )
```

time: 135 us -> 119 us (0.88)
  blocking collectives: 54.9 us -> 0 us
  waiting for transfers between devices: 29.4 us -> 55.3 us
  starting transfers between devices: 8.38 us -> 27.8 us
  Pallas kernels: 37 us -> 31.2 us
  other arithmetic: 1.57 us -> 0.01 us
    all_to_all x2 -> x0, blocking collectives: 54.9 us -> none  [the longest x1 34.3 us: local(): shares = lax.all_to_all(share, 'shard', 0, 0, tiled=True)]
    all_to_all x0 -> x2, waiting for transfers between devices: none -> 31.5 us  [the longest x1 24.1 us: local(): shares = lax.all_to_all(share, 'shard', 0, 0, tiled=True)]
    all_to_all x0 -> x2, starting transfers between devices: none -> 18.7 us  [the longest x1 12 us: local(): asked = lax.all_to_all(code, 'shard', 0, 0, tiled=True)]
    pallas_call x5 -> x8, Pallas kernels: 37 us -> 31.2 us  [call(): pl.pallas_call(body, out_shape=out_shape, in_specs=[hbm if n in in_hbm el...]
    all_to_all x1, waiting for transfers between devices: 26.9 us -> 21.3 us  [local(): got = lax.all_to_all(found, 'shard', 0, 0, tiled=True)]
    unnamed x6 -> x24, local copies, waits for them, and re-layouts: 2.32 us -> 2.87 us
  transfers between devices with their start and end apart: 2 -> 4, of which waited for: 2 -> 4; matrix products, arithmetic and copies ran while one was open for 0% -> 0% of each run, Pallas kernels for 0% -> 8%
where the time goes in v2:
time: 119 us; the launch traced here: 118 us
  waiting for transfers between devices  55.3 us (46%)
  Pallas kernels  31.2 us (26%)
  starting transfers between devices  27.8 us (23%)
  local copies, waits for them, and re-layouts  2.87 us (2%)
    pallas_call x8, Pallas kernels, call(): pl.pallas_call(body, out_shape=out_shape, in_specs=[hbm if n in in_hbm el...  31.2 us
    all_to_all x1, waiting for transfers between devices, local(): shares = lax.all_to_all(share, 'shard', 0, 0, tiled=True)  24.1 us
    all_to_all x1, waiting for transfers between devices, local(): got = lax.all_to_all(found, 'shard', 0, 0, tiled=True)  21.3 us
    all_to_all x1, starting transfers between devices, local(): asked = lax.all_to_all(code, 'shard', 0, 0, tiled=True)  12 us
    all_to_all x1, waiting for transfers between devices, local(): asked = lax.all_to_all(code, 'shard', 0, 0, tiled=True)  7.44 us
    all_to_all x1, starting transfers between devices, local(): shares = lax.all_to_all(share, 'shard', 0, 0, tiled=True)  6.7 us
    all_to_all x1, starting transfers between devices, local(): got = lax.all_to_all(found, 'shard', 0, 0, tiled=True)  5.71 us
    ppermute x1, starting transfers between devices, local(): peer = lax.ppermute(mine, 'replica', [(0, 1), (1, 0)])  3.42 us
  transfers between devices with their start and end apart: 4, of which 4 were waited for; matrix products, arithmetic and copies ran while one was open for 0% of the time, Pallas kernels for 8%

profile of v2, /device:TPU:1, one launch (start us, length us, event | category | flops | bytes accessed | tf_op | source)
XLA Modules:
  0.0 118.0 jit_solution(8487106527024217320)
XLA Ops:
  0.6 3.7 %shard_map.130 = (bf16[64,8,128]{2,1,0:T(8,128)(2,1)}, bf16[2,64,512]{2,1,0:T(8,128)(2,1)}) custom-call(s32[2,16,128]{2,1,0:T(8,128)} %bitcast.29, s32[2,128]{1,0:T(2,128)} %bitcast.34), custom_call_target="tpu_custom_call" | custom-call | tf_op jit(solution)/shard_map/pallas_call | solution.py:331
  4.3 12.0 %all-to-all-start = ((bf16[64,8,128]{2,1,0:T(8,128)(2,1)}), bf16[64,8,128]{2,1,0:T(8,128)(2,1)S(1)}, u32[]{:S(2)}, u32[]{:S(2)}) async-start(bf16[64,8,128]{2,1,0:T(8,128)(2,1)} %get-tuple-element.11), calls=%async_computation | async-start | bytes 262144 | tf_op jit(solution)/shard_map/all_to_all | solution.py:378
  16.3 0.0 copy-start.2
  16.3 1.2 %copy-done.2 = f32[512,2,256]{2,1,0:T(2,128)S(1)} copy-done((f32[512,2,256]{2,1,0:T(2,128)S(1)}, f32[512,2,256]{2,1,0:T(2,128)}, u32[]{:S(2)}) %copy-start.2) | copy-done | bytes 1048600
  17.5 0.1 shard_map.132.low_ref
  17.6 7.4 %all-to-all-done.code_ref = bf16[64,8,128]{2,1,0:T(8,128)(2,1)S(1)} async-done(((bf16[64,8,128]{2,1,0:T(8,128)(2,1)}), bf16[64,8,128]{2,1,0:T(8,128)(2,1)S(1)}, u32[]{:S(2)}, u32[]{:S(2)}) %all-to-all-start) | async-done | bytes 131104 | tf_op jit(solution)/shard_map/all_to_all | solution.py:378
  25.0 3.3 %shard_map.133 = bf16[64,64,256]{2,1,0:T(8,128)(2,1)} custom-call(bf16[64,8,128]{2,1,0:T(8,128)(2,1)S(1)} %all-to-all-done.code_ref, bf16[2,512,256]{2,1,0:T(8,128)(2,1)S(1)} %shard_map.132.low_ref), custom_call_target="tpu_custom_call" | custom-call | tf_op jit(solution)/shard_map/pallas_call | solution.py:331
  28.4 0.0 copy-start.11
  28.4 0.0 copy-start.4
  28.4 0.0 copy-start.6
  28.4 0.0 copy-start.7
  28.4 0.0 copy-start.9
  28.4 0.0 copy-start.1
  28.4 0.0 copy-start.5
  28.4 0.0 copy-start.10
  28.5 5.7 %all-to-all-start.1 = ((bf16[64,64,256]{2,1,0:T(8,128)(2,1)}), bf16[64,64,256]{2,1,0:T(8,128)(2,1)}, u32[]{:S(2)}, u32[]{:S(2)}) async-start(bf16[64,64,256]{2,1,0:T(8,128)(2,1)} %shard_map.133), calls=%async_computation.1 | async-start | bytes 4194304 | tf_op jit(solution)/shard_map/all_to_all | solution.py:399
  34.2 0.0 copy-done.11
  34.2 0.0 copy-done.4
  34.2 0.0 copy-done.6
  34.2 0.0 copy-done.7
  34.2 0.0 copy-done.9
  34.2 6.0 %shard_map.131.ct_ref = bf16[2,2048,128]{2,1,0:T(8,128)(2,1)S(1)} custom-call(s32[2,16,128]{2,1,0:T(8,128)S(1)} %bitcast.30, s32[2,128]{1,0:T(2,128)S(1)} %bitcast.35, bf16[2,16,128]{2,1,0:T(8,128)(2,1)S(1)} %bitcast.32, bf16[2,64,512]{2,1,0:T(8,128)(2,1)S(1)} %copy-done.4), custom_call_target="tpu_custom_call" | custom-call | tf_op jit(solution)/shard_map/pallas_call | solution.py:331
  40.3 21.3 %all-to-all-done.1.got_ref = bf16[64,64,256]{2,1,0:T(8,128)(2,1)} async-done(((bf16[64,64,256]{2,1,0:T(8,128)(2,1)}), bf16[64,64,256]{2,1,0:T(8,128)(2,1)}, u32[]{:S(2)}, u32[]{:S(2)}) %all-to-all-start.1) | async-done | bytes 2097184 | tf_op jit(solution)/shard_map/all_to_all | solution.py:399
  61.6 0.0 copy-done.1
  61.6 0.0 copy-done.5
  61.6 0.0 copy-done.10
  61.6 11.2 %shard_map.134 = bf16[64,64,256]{2,1,0:T(8,128)(2,1)} custom-call(bf16[2,2048,128]{2,1,0:T(8,128)(2,1)S(1)} %shard_map.131.ct_ref, bf16[64,64,256]{2,1,0:T(8,128)(2,1)} %all-to-all-done.1.got_ref, bf16[128,256]{1,0:T(8,128)(2,1)S(1)} %copy-done.5, s32[1,128]{1,0:T(1,128)S(1)} %bitcast.36, f32[1,4096]{1,0:T(1,128)S(1)} %bitcast.31, ...), custom_call_target="tpu_custom_call" | custom-call | tf_op jit(solution)/shard_map/pallas_call | solution.py:331
  72.8 0.0 copy-start.8
  72.8 6.7 %all-to-all-start.2 = ((bf16[64,64,256]{2,1,0:T(8,128)(2,1)}), bf16[64,64,256]{2,1,0:T(8,128)(2,1)S(1)}, u32[]{:S(2)}, u32[]{:S(2)}) async-start(bf16[64,64,256]{2,1,0:T(8,128)(2,1)} %shard_map.134), calls=%async_computation.2 | async-start | bytes 4194304 | tf_op jit(solution)/shard_map/all_to_all | solution.py:433
  79.5 0.0 copy-done.8
  79.5 3.4 %shard_map.135 = (f8e4m3fn[2,512,2048]{2,1,0:T(32,128)(4,1)}, f32[128,128]{1,0:T(8,128)S(1)}) custom-call(bf16[64,8,128]{2,1,0:T(8,128)(2,1)S(1)} %all-to-all-done.code_ref, f32[2,512]{1,0:T(2,128)S(1)} %bitcast.33), custom_call_target="tpu_custom_call" | custom-call | tf_op jit(solution)/shard_map/pallas_call | solution.py:331
  82.9 24.1 %all-to-all-done.2.share_ref = bf16[64,64,256]{2,1,0:T(8,128)(2,1)S(1)} async-done(((bf16[64,64,256]{2,1,0:T(8,128)(2,1)}), bf16[64,64,256]{2,1,0:T(8,128)(2,1)S(1)}, u32[]{:S(2)}, u32[]{:S(2)}) %all-to-all-start.2) | async-done | bytes 2097184 | tf_op jit(solution)/shard_map/all_to_all | solution.py:433
  107.0 0.0 copy-start
  107.0 1.6 %copy-done = f8e4m3fn[2,512,2048]{2,1,0:T(32,128)(4,1)S(1)} copy-done((f8e4m3fn[2,512,2048]{2,1,0:T(32,128)(4,1)S(1)}, f8e4m3fn[2,512,2048]{2,1,0:T(32,128)(4,1)}, u32[]{:S(2)}) %copy-start) | copy-done | bytes 2097176
  108.5 0.0 copy-start.3
  108.6 1.6 %shard_map.136.mine_ref = f32[1152,256]{1,0:T(8,128)S(1)} custom-call(f8e4m3fn[2,512,2048]{2,1,0:T(32,128)(4,1)S(1)} %copy-done, f32[128,128]{1,0:T(8,128)S(1)} %get-tuple-element.15.columns_ref, bf16[64,64,256]{2,1,0:T(8,128)(2,1)S(1)} %all-to-all-done.2.share_ref), custom_call_target="tpu_custom_call" | custom-call | tf_op jit(solution)/shard_map/pallas_call | solution.py:331
  110.1 3.4 %collective-permute-start = (f32[1152,256]{1,0:T(8,128)S(1)}, f32[1152,256]{1,0:T(8,128)S(1)}, u32[]{:S(2)}, u32[]{:S(2)}) collective-permute-start(f32[1152,256]{1,0:T(8,128)S(1)} %shard_map.136.mine_ref), channel_id=1, source_target_pairs={{0,64},{64,0},{1,65},{65,1},{2,66},{66,2},{3,67},{67,3},{4,68},{68... | collective-permute-start | bytes 3538952 | tf_op jit(solution)/shard_map/ppermute | solution.py:452
  113.6 2.5 %collective-permute-done.peer_ref = f32[1152,256]{1,0:T(8,128)S(1)} collective-permute-done((f32[1152,256]{1,0:T(8,128)S(1)}, f32[1152,256]{1,0:T(8,128)S(1)}, u32[]{:S(2)}, u32[]{:S(2)}) %collective-permute-start) | collective-permute-done | bytes 1179680 | tf_op jit(solution)/shard_map/ppermute | solution.py:452
  116.0 0.0 copy-done.3
  116.0 2.0 %shard_map.137 = (f32[2048,128]{1,0:T(8,128)}, f32[2,512]{1,0:T(2,128)}, f32[2048,128]{1,0:T(8,128)}) custom-call(f32[1152,256]{1,0:T(8,128)S(1)} %shard_map.136.mine_ref, f32[1152,256]{1,0:T(8,128)S(1)} %collective-permute-done.peer_ref, f32[2048,128]{1,0:T(8,128)S(1)} %bitcast.28), custom_call_target="tpu_custom_call" | custom-call | tf_op jit(solution)/shard_map/pallas_call | solution.py:331
  (1 shorter events, 0.0 us)
Async XLA Ops:
  4.3 20.8 %all-to-all-start = ((bf16[64,8,128]{2,1,0:T(8,128)(2,1)}), bf16[64,8,128]{2,1,0:T(8,128)(2,1)S(1)}, u32[]{:S(2)}, u32[]{:S(2)}) async-start(bf16[64,8,128]{2,1,0:T(8,128)(2,1)} %get-tuple-element.11), calls=%async_computation | async-start | bytes 262144 | tf_op jit(solution)/shard_map/all_to_all | solution.py:378
  16.3 1.2 %copy-start.2 = (f32[512,2,256]{2,1,0:T(2,128)S(1)}, f32[512,2,256]{2,1,0:T(2,128)}, u32[]{:S(2)}) copy-start(f32[512,2,256]{2,1,0:T(2,128)} %param.16) | copy-start | bytes 3145732
  28.4 5.8 %copy-start.11 = (bf16[4096]{0:T(1024)(128)(2,1)S(1)}, bf16[4096]{0:T(1024)(128)(2,1)}, u32[]{:S(2)}) copy-start(bf16[4096]{0:T(1024)(128)(2,1)} %param.21) | copy-start | bytes 24580
  28.4 5.8 %copy-start.4 = (bf16[2,64,512]{2,1,0:T(8,128)(2,1)S(1)}, bf16[2,64,512]{2,1,0:T(8,128)(2,1)}, u32[]{:S(2)}) copy-start(bf16[2,64,512]{2,1,0:T(8,128)(2,1)} %get-tuple-element.12.rank_ref) | copy-start | bytes 393220
  28.4 5.8 %copy-start.6 = (s32[128,2,16]{0,2,1:T(8,128)S(1)}, s32[128,2,16]{0,2,1:T(8,128)}, u32[]{:S(2)}) copy-start(s32[128,2,16]{0,2,1:T(8,128)} %param.12) | copy-start | bytes 49156
  28.4 5.8 %copy-start.7 = (bf16[128,2,16]{0,2,1:T(8,128)(2,1)S(1)}, bf16[128,2,16]{0,2,1:T(8,128)(2,1)}, u32[]{:S(2)}) copy-start(bf16[128,2,16]{0,2,1:T(8,128)(2,1)} %param.14) | copy-start | bytes 24580
  28.4 5.8 %copy-start.9 = (s32[128,2]{0,1:T(2,128)S(1)}, s32[128,2]{0,1:T(2,128)}, u32[]{:S(2)}) copy-start(s32[128,2]{0,1:T(2,128)} %param.13) | copy-start | bytes 3076
  28.4 33.2 %copy-start.1 = (bf16[768,768]{1,0:T(8,128)(2,1)S(1)}, bf16[768,768]{1,0:T(8,128)(2,1)}, u32[]{:S(2)}) copy-start(bf16[768,768]{1,0:T(8,128)(2,1)} %cross_hbm.1) | copy-start | bytes 3538948
  28.4 33.2 %copy-start.5 = (bf16[128,256]{1,0:T(8,128)(2,1)S(1)}, bf16[128,256]{1,0:T(8,128)(2,1)}, u32[]{:S(2)}) copy-start(bf16[128,256]{1,0:T(8,128)(2,1)} %dense_ref.1) | copy-start | bytes 196612
  28.4 33.1 %copy-start.10 = (s32[128]{0:T(128)S(1)}, s32[128]{0:T(128)}, u32[]{:S(2)}) copy-start(s32[128]{0:T(128)} %param.15) | copy-start | bytes 1540
  28.5 33.1 %all-to-all-start.1 = ((bf16[64,64,256]{2,1,0:T(8,128)(2,1)}), bf16[64,64,256]{2,1,0:T(8,128)(2,1)}, u32[]{:S(2)}, u32[]{:S(2)}) async-start(bf16[64,64,256]{2,1,0:T(8,128)(2,1)} %shard_map.133), calls=%async_computation.1 | async-start | bytes 4194304 | tf_op jit(solution)/shard_map/all_to_all | solution.py:399
  72.8 6.7 %copy-start.8 = (f32[512,2]{0,1:T(2,128)S(1)}, f32[512,2]{0,1:T(2,128)}, u32[]{:S(2)}) copy-start(f32[512,2]{0,1:T(2,128)} %param.18) | copy-start | bytes 12292
  72.8 34.2 %all-to-all-start.2 = ((bf16[64,64,256]{2,1,0:T(8,128)(2,1)}), bf16[64,64,256]{2,1,0:T(8,128)(2,1)S(1)}, u32[]{:S(2)}, u32[]{:S(2)}) async-start(bf16[64,64,256]{2,1,0:T(8,128)(2,1)} %shard_map.134), calls=%async_computation.2 | async-start | bytes 4194304 | tf_op jit(solution)/shard_map/all_to_all | solution.py:433
  107.0 1.6 %copy-start = (f8e4m3fn[2,512,2048]{2,1,0:T(32,128)(4,1)S(1)}, f8e4m3fn[2,512,2048]{2,1,0:T(32,128)(4,1)}, u32[]{:S(2)}) copy-start(f8e4m3fn[2,512,2048]{2,1,0:T(32,128)(4,1)} %get-tuple-element.14.hot_ref) | copy-start | bytes 6291460
  108.5 7.5 %copy-start.3 = (f32[512,2,256]{2,1,0:T(2,128)S(1)}, f32[512,2,256]{2,1,0:T(2,128)}, u32[]{:S(2)}) copy-start(f32[512,2,256]{2,1,0:T(2,128)} %param.17) | copy-start | bytes 3145732
  110.1 5.9 %collective-permute-start = (f32[1152,256]{1,0:T(8,128)S(1)}, f32[1152,256]{1,0:T(8,128)S(1)}, u32[]{:S(2)}, u32[]{:S(2)}) collective-permute-start(f32[1152,256]{1,0:T(8,128)S(1)} %shard_map.136.mine_ref), channel_id=1, source_target_pairs={{0,64},{64,0},{1,65},{65,1},{2,66},{66,2},{3,67},{67,3},{4,68},{68... | collective-permute-start | bytes 3538952 | tf_op jit(solution)/shard_map/ppermute | solution.py:452

commit v3 on v2

--- a/solution.py
+++ b/solution.py
@@ -66,9 +66,9 @@
         loc = (rows & (own_rows - 1)).astype(F32)
         for l in range(slots):
             cols = slice(l * samples, (l + 1) * samples)
-            own_hot[:, cols] = ones_where(owner_ids == own[l : l + 1, :])
-            fill_row_hot(row_hot, l, loc[l : l + 1, :])
-        present = dot(own_hot[...], row_hot[...], NT) > 0.0
+            own_hot[t, :, cols] = ones_where(owner_ids == own[l : l + 1, :])
+            fill_row_hot(row_hot.at[t], l, loc[l : l + 1, :])
+        present = dot(own_hot[t], row_hot[t], NT) > 0.0
         rank = dot(ones_where(present), before)
         code = jnp.where(present, rank, -1.0)
         for c in range(pieces):
@@ -131,61 +131,74 @@
     devices = code_ref.shape[0]
     tables = low_ref.shape[0]
     pieces = code_ref.shape[1] // tables
-    group = hot.shape[1] // CAP
+    group = hot.shape[2] // CAP
+    steps = devices // group
     rank_ids = iota((CAP, LANES), 0).astype(F32).astype(BF16)
 
-    def body(step, _):
+    def send(step):
+        block = pl.ds(step * group, group)
+        return pltpu.make_async_copy(out.at[block], out_hbm.at[block], sems.at[step])
+
+    for step in range(steps):
         first = step * group
+        slot = hot.at[step % 2]
         for d in range(group):
             codes = code_ref[first + d].astype(F32)
             for t in range(tables):
                 for c, part in enumerate(hot_rows(codes, rank_ids, t, pieces)):
-                    hot[t, d * CAP : (d + 1) * CAP, c * LANES : (c + 1) * LANES] = part
+                    slot[t, d * CAP : (d + 1) * CAP, c * LANES : (c + 1) * LANES] = part
         for t in range(tables):
-            got = dot(hot[t], low_ref[t]).astype(BF16)
-            out[pl.ds(first, group), t * CAP : (t + 1) * CAP, :] = got.reshape(group, CAP, -1)
+            got = dot(slot[t], low_ref[t]).astype(BF16)
+            out[first : first + group, t * CAP : (t + 1) * CAP, :] = got.reshape(group, CAP, -1)
         send(step).start()
-        return 0
-
-    def send(step):
-        block = pl.ds(step * group, group)
-        return pltpu.make_async_copy(out.at[block], out_hbm.at[block], sems.at[step])
-
-    steps = devices // group
-    lax.fori_loop(0, steps, body, 0)
     for step in range(steps):
         send(step).wait()
 
 
 def dense_kernel(
-    ct_ref, got_ref, dense_ref, labels_ref, head_ref, cross_hbm, hidden_hbm, out_hbm,
-    cross, hidden_w, joined, before, out, sems, out_sems,
+    ct_ref, dense_ref, labels_ref, head_ref, got_hbm, cross_hbm, hidden_hbm, out_hbm,
+    got, cross, hidden_w, joined, before, out_grad, out, sems, out_sems,
 ):
     tables, spots, samples = ct_ref.shape
     owners = spots // CAP
     width = dense_ref.shape[1]
-    copy_cross = pltpu.make_async_copy(cross_hbm, cross, sems.at[0])
-    copy_hidden = pltpu.make_async_copy(hidden_hbm, hidden_w, sems.at[1])
-    copy_cross.start()
-    copy_hidden.start()
+    units = hidden_w.shape[1]
+    chunk = 1024
+    take_got = [
+        pltpu.make_async_copy(got_hbm.at[:, pl.ds(t * CAP, CAP), :], got.at[t], sems.at[t])
+        for t in range(tables)
+    ]
+    take_cross = pltpu.make_async_copy(cross_hbm, cross, sems.at[tables])
+    take_hidden = [
+        pltpu.make_async_copy(
+            hidden_hbm.at[:, pl.ds(n * chunk, chunk)],
+            hidden_w.at[:, pl.ds(n * chunk, chunk)],
+            sems.at[tables + 1 + n],
+        )
+        for n in range(units // chunk)
+    ]
+    for copy in take_got + [take_cross] + take_hidden:
+        copy.start()
     joined[:, :width] = dense_ref[...]
     for t in range(tables):
-        got = got_ref[:, t * CAP : (t + 1) * CAP, :].reshape(spots, width)
-        joined[:, (t + 1) * width : (t + 2) * width] = dot(ct_ref[t], got, TN).astype(BF16)
-    copy_cross.wait()
+        take_got[t].wait()
+        rows = got[t].reshape(spots, width)
+        joined[:, (t + 1) * width : (t + 2) * width] = dot(ct_ref[t], rows, TN).astype(BF16)
+    take_cross.wait()
     widened = joined[...].astype(F32)
     crossed = dot(joined[...], cross[...])
     layered = (widened * crossed + widened).astype(BF16)
-    copy_hidden.wait()
-    units = hidden_w.shape[1]
-    chunk = 512
-    logits = jnp.zeros((samples, 1), F32)
+    logits = jnp.zeros((samples, LANES), F32)
     for n in range(units // chunk):
         cols = slice(n * chunk, (n + 1) * chunk)
+        take_hidden[n].wait()
         part = dot(layered, hidden_w[:, cols])
         before[:, cols] = part
         active = jnp.maximum(part, 0.0).astype(BF16).astype(F32)
-        logits = logits + jnp.sum(active * head_ref[:, cols], axis=1, keepdims=True)
+        active = active * head_ref[:, cols]
+        for m in range(chunk // LANES):
+            logits = logits + active[:, m * LANES : (m + 1) * LANES]
+    logits = jnp.sum(logits, axis=1, keepdims=True)
     diagonal = iota((samples, samples), 0) == iota((samples, samples), 1)
     marks = jnp.sum(
         jnp.where(diagonal, labels_ref[...].astype(F32), 0.0), axis=1, keepdims=True
@@ -194,16 +207,18 @@
     back = jnp.zeros((samples, layered.shape[1]), F32)
     for n in range(units // chunk):
         cols = slice(n * chunk, (n + 1) * chunk)
-        grad = jnp.where(before[:, cols] > 0.0, slope * head_ref[:, cols], 0.0).astype(BF16)
-        back = back + dot(grad, hidden_w[:, cols], NT)
+        out_grad[:, cols] = jnp.where(
+            before[:, cols] > 0.0, slope * head_ref[:, cols], 0.0
+        ).astype(BF16)
+    back = dot(out_grad[...], hidden_w[...], NT)
     mixed = (back * widened).astype(BF16)
-    steps = out_sems.shape[0]
+    steps = out_sems.shape[1]
     part_rows = spots // steps
     part_owners = owners // steps
 
-    def send(n):
-        block = pl.ds(n * part_owners, part_owners)
-        return pltpu.make_async_copy(out.at[block], out_hbm.at[block], out_sems.at[n])
+    def send(t, n):
+        block = (pl.ds(n * part_owners, part_owners), pl.ds(t * CAP, CAP))
+        return pltpu.make_async_copy(out.at[block], out_hbm.at[block], out_sems.at[t, n])
 
     for t in range(tables):
         cols = slice((t + 1) * width, (t + 2) * width)
@@ -213,13 +228,14 @@
             share = dot(ct_ref[t, n * part_rows : (n + 1) * part_rows, :], grads).astype(BF16)
             block = slice(n * part_owners, (n + 1) * part_owners)
             out[block, t * CAP : (t + 1) * CAP, :] = share.reshape(part_owners, CAP, width)
-            if t == tables - 1:
-                send(n).start()
-    for n in range(steps):
-        send(n).wait()
-
-
-def spread_kernel(tables, code_ref, second_ref, hot_ref, columns_ref, tall):
+            send(t, n).start()
+    for t in range(tables):
+        for n in range(steps):
+            send(t, n).wait()
+
+
+def spread_kernel(tables, code_ref, second_ref, *refs):
+    hot_refs, (columns_ref, tall) = refs[:tables], refs[tables:]
     devices = code_ref.shape[0]
     pieces = code_ref.shape[1] // tables
     count = tables * pieces
@@ -233,8 +249,8 @@
             parts = [hot_rows(code, rank_ids, t, pieces) for code in codes]
             for c in range(pieces):
                 block = jnp.concatenate([part[c] for part in parts], axis=0)
-                hot_ref[
-                    t, c * LANES : (c + 1) * LANES, pl.ds(pl.multiple_of(step * LANES, LANES), LANES)
+                hot_refs[t][
+                    c * LANES : (c + 1) * LANES, pl.ds(pl.multiple_of(step * LANES, LANES), LANES)
                 ] = jnp.transpose(block).astype(HOT)
         for code in codes:
             top = jnp.maximum(top, code)
@@ -250,67 +266,62 @@
     columns_ref[...] = jnp.transpose(tall[...])
 
 
-def collect_kernel(hot_ref, columns_ref, share_ref, out_ref):
-    tables, own_rows, spots = hot_ref.shape
+def collect_kernel(t, tables, hot_ref, columns_ref, share_ref, out_ref):
+    own_rows, spots = hot_ref.shape
     width = share_ref.shape[2]
     pieces = own_rows // LANES
-    count = tables * pieces
     lane_ids = iota((LANES, LANES), 1)
     stats = jnp.zeros((LANES, LANES), F32)
-    for t in range(tables):
-        shares = share_ref[:, t * CAP : (t + 1) * CAP, :].reshape(spots, width)
-        for c in range(pieces):
-            at = t * pieces + c
-            grad = dot(hot_ref[t, c * LANES : (c + 1) * LANES, :].astype(BF16), shares)
-            touched = columns_ref[:, at : at + 1] >= 0.0
-            second = columns_ref[:, count + at : count + at + 1]
-            mean = jnp.mean(grad * grad, axis=1, keepdims=True)
-            second = jnp.where(
-                touched, beta_second * second + (1.0 - beta_second) * mean, second
-            )
-            scale = jnp.where(touched, 1.0 / (jnp.sqrt(second) + epsilon), 0.0)
-            decay = jnp.where(touched, beta_first, 1.0)
-            stats = jnp.where(lane_ids == at, second, stats)
-            stats = jnp.where(lane_ids == count + at, scale, stats)
-            stats = jnp.where(lane_ids == 2 * count + at, decay, stats)
-            out_ref[at * LANES : (at + 1) * LANES, :] = (1.0 - beta_first) * grad
-    out_ref[count * LANES :, :LANES] = stats
-    out_ref[count * LANES :, LANES:] = jnp.zeros((LANES, width - LANES), F32)
-
-
-def adam_kernel(mine_ref, peer_ref, first_ref, first_out, second_out, step_out):
-    tables, own_rows = second_out.shape
-    width = mine_ref.shape[1]
+    shares = share_ref[:, t * CAP : (t + 1) * CAP, :].reshape(spots, width)
+    for c in range(pieces):
+        at = t * pieces + c
+        grad = dot(hot_ref[c * LANES : (c + 1) * LANES, :].astype(BF16), shares)
+        touched = columns_ref[:, at : at + 1] >= 0.0
+        at = at + tables * pieces
+        second = columns_ref[:, at : at + 1]
+        mean = jnp.mean(grad * grad, axis=1, keepdims=True)
+        second = jnp.where(touched, beta_second * second + (1.0 - beta_second) * mean, second)
+        scale = jnp.where(touched, 1.0 / (jnp.sqrt(second) + epsilon), 0.0)
+        decay = jnp.where(touched, beta_first, 1.0)
+        stats = jnp.where(lane_ids == c, second, stats)
+        stats = jnp.where(lane_ids == pieces + c, scale, stats)
+        stats = jnp.where(lane_ids == 2 * pieces + c, decay, stats)
+        out_ref[c * LANES : (c + 1) * LANES, :] = (1.0 - beta_first) * grad
+    out_ref[own_rows:, :LANES] = stats
+    out_ref[own_rows:, LANES:] = jnp.zeros((LANES, width - LANES), F32)
+
+
+def adam_kernel(tables, *refs):
+    mine_refs, peer_refs = refs[:tables], refs[tables : 2 * tables]
+    first_ref, first_out, second_out, step_out = refs[2 * tables :]
+    own_rows = second_out.shape[1]
+    width = mine_refs[0].shape[1]
     pieces = own_rows // LANES
     halves = width // LANES
-    count = tables * pieces
-    mine = mine_ref[count * LANES :, :LANES]
-    peer = peer_ref[count * LANES :, :LANES]
-    second_all = jnp.transpose((mine + peer) * 0.5)
-    for t in range(tables):
+    for t in range(tables):
+        pair = (mine_refs[t], peer_refs[t])
+        stats = [ref[own_rows:, :LANES] for ref in pair]
+        second = jnp.transpose((stats[0] + stats[1]) * 0.5)
         for c in range(pieces):
-            at = t * pieces + c
-            rows = slice(at * LANES, (at + 1) * LANES)
-            second_out[t : t + 1, c * LANES : (c + 1) * LANES] = second_all[at : at + 1, :]
-            sides = [
-                (
-                    ref,
-                    jnp.broadcast_to(s[:, 2 * count + at : 2 * count + at + 1], (LANES, LANES)),
-                    jnp.broadcast_to(s[:, count + at : count + at + 1] * 0.5, (LANES, LANES)),
-                )
-                for ref, s in ((mine_ref, mine), (peer_ref, peer))
+            rows = slice(c * LANES, (c + 1) * LANES)
+            second_out[t : t + 1, rows] = second[c : c + 1, :]
+            scales = [
+                jnp.broadcast_to(s[:, pieces + c : pieces + c + 1] * 0.5, (LANES, LANES))
+                for s in stats
+            ]
+            decays = [
+                jnp.broadcast_to(s[:, 2 * pieces + c : 2 * pieces + c + 1], (LANES, LANES))
+                for s in stats
             ]
             for h in range(halves):
                 view = pl.ds(
-                    c * LANES * count // pieces * halves + h * tables + t,
-                    LANES,
-                    stride=tables * halves,
+                    c * LANES * tables * halves + h * tables + t, LANES, stride=tables * halves
                 )
                 first = first_ref[view, :]
                 cols = slice(h * LANES, (h + 1) * LANES)
-                firsts = [decay * first + ref[rows, cols] for ref, decay, _ in sides]
+                firsts = [decay * first + ref[rows, cols] for decay, ref in zip(decays, pair)]
                 first_out[view, :] = (firsts[0] + firsts[1]) * 0.5
-                step_out[view, :] = firsts[0] * sides[0][2] + firsts[1] * sides[1][2]
+                step_out[view, :] = firsts[0] * scales[0] + firsts[1] * scales[1]
 
 
 def to_rows(x):
@@ -368,8 +379,8 @@
             shape((tables, owners, own_rows), BF16),
         ),
         [
-            pltpu.VMEM((owners, slots * samples), BF16),
-            pltpu.VMEM((own_rows, slots * samples), BF16),
+            pltpu.VMEM((tables, owners, slots * samples), BF16),
+            pltpu.VMEM((tables, own_rows, slots * samples), BF16),
             pltpu.VMEM((owners, count, LANES), F32),
         ],
         rows,
@@ -388,7 +399,7 @@
         50,
         shape((owners, tables * CAP, width), BF16),
         [
-            pltpu.VMEM((tables, GROUP * CAP, own_rows), BF16),
+            pltpu.VMEM((2, tables, GROUP * CAP, own_rows), BF16),
             pltpu.VMEM((owners, tables * CAP, width), BF16),
             pltpu.SemaphoreType.DMA((owners // GROUP,)),
         ],
@@ -412,46 +423,52 @@
         50,
         shape((owners, tables * CAP, width), BF16),
         [
+            pltpu.VMEM((tables, owners, CAP, width), BF16),
             pltpu.VMEM(cross_weight.shape, BF16),
             pltpu.VMEM(hidden_weight.shape, BF16),
             pltpu.VMEM((samples, cross_weight.shape[0]), BF16),
             pltpu.VMEM((samples, hidden_weight.shape[1]), F32),
+            pltpu.VMEM((samples, hidden_weight.shape[1]), BF16),
             pltpu.VMEM((owners, tables * CAP, width), BF16),
-            pltpu.SemaphoreType.DMA((2,)),
-            pltpu.SemaphoreType.DMA((4,)),
+            pltpu.SemaphoreType.DMA((tables + 1 + hidden_weight.shape[1] // 1024,)),
+            pltpu.SemaphoreType.DMA((tables, 4)),
         ],
         ct,
-        got,
         dense_input,
         labels.reshape(1, samples),
         head_weight.astype(F32).reshape(1, -1),
+        got,
         cross_weight,
         hidden_weight,
-        in_hbm=(5, 6),
+        in_hbm=(4, 5, 6),
         out_hbm=True,
     )
     shares = lax.all_to_all(share, "shard", 0, 0, tiled=True)
     asked_later, _ = lax.optimization_barrier((asked, share))
-    hot, columns = call(
+    *hots, columns = call(
         functools.partial(spread_kernel, tables),
         52,
-        (shape((tables, own_rows, spots), HOT), shape((LANES, LANES), F32)),
+        tuple(shape((own_rows, spots), HOT) for _ in range(tables))
+        + (shape((LANES, LANES), F32),),
         [pltpu.VMEM((LANES, LANES), F32)],
         asked_later,
         jnp.transpose(second_moment),
     )
-    mine = call(
-        collect_kernel,
-        14,
-        shape((count * LANES + LANES, width), F32),
-        [],
-        hot,
-        columns,
-        shares,
-    )
-    peer = lax.ppermute(mine, "replica", [(0, 1), (1, 0)])
+    mine, peer = [], []
+    for t in range(tables):
+        part = call(
+            functools.partial(collect_kernel, t, tables),
+            14,
+            shape((own_rows + LANES, width), F32),
+            [],
+            hots[t],
+            columns,
+            shares,
+        )
+        mine.append(part)
+        peer.append(lax.ppermute(part, "replica", [(0, 1), (1, 0)]))
     first, second, step = call(
-        adam_kernel,
+        functools.partial(adam_kernel, tables),
         12,
         (
             shape((own_rows * tables * width // LANES, LANES), F32),
@@ -459,8 +476,8 @@
             shape((own_rows * tables * width // LANES, LANES), F32),
         ),
         [],
-        mine,
-        peer,
+        *mine,
+        *peer,
         to_rows(first_moment),
     )
     return (

time: 119 us -> 115 us (0.966)
  Pallas kernels: 31.2 us -> 28 us
    pallas_call x8 -> x9, Pallas kernels: 31.2 us -> 28 us  [call(): pl.pallas_call(body, out_shape=out_shape, in_specs=[hbm if n in in_hbm el...]
    ppermute x1 -> x2, waiting for transfers between devices: 2.47 us -> 2.08 us  [local(): peer.append(lax.ppermute(part, 'replica', [(0, 1), (1, 0)]))]
    ppermute x1 -> x2, starting transfers between devices: 3.42 us -> 3.49 us  [local(): peer.append(lax.ppermute(part, 'replica', [(0, 1), (1, 0)]))]
  transfers between devices with their start and end apart: 4 -> 5, of which waited for: 4 -> 5; matrix products, arithmetic and copies ran while one was open for 0% -> 0% of each run, Pallas kernels for 8% -> 9%
where the time goes in v3:
time: 115 us
  waiting for transfers between devices  55.5 us (48%)
  Pallas kernels  28 us (24%)
  starting transfers between devices  27.7 us (24%)
  local copies, waits for them, and re-layouts  2.51 us (2%)
    pallas_call x9, Pallas kernels, call(): pl.pallas_call(body, out_shape=out_shape, in_specs=[hbm if n in in_hbm el...  28 us
    all_to_all x1, waiting for transfers between devices, local(): shares = lax.all_to_all(share, 'shard', 0, 0, tiled=True)  24.6 us
    all_to_all x1, waiting for transfers between devices, local(): got = lax.all_to_all(found, 'shard', 0, 0, tiled=True)  21.3 us
    all_to_all x1, starting transfers between devices, local(): asked = lax.all_to_all(code, 'shard', 0, 0, tiled=True)  12 us
    all_to_all x1, waiting for transfers between devices, local(): asked = lax.all_to_all(code, 'shard', 0, 0, tiled=True)  7.44 us
    all_to_all x1, starting transfers between devices, local(): shares = lax.all_to_all(share, 'shard', 0, 0, tiled=True)  6.54 us
    all_to_all x1, starting transfers between devices, local(): got = lax.all_to_all(found, 'shard', 0, 0, tiled=True)  5.71 us
    ppermute x2, starting transfers between devices, local(): peer.append(lax.ppermute(part, 'replica', [(0, 1), (1, 0)]))  3.49 us
  transfers between devices with their start and end apart: 5, of which 5 were waited for; matrix products, arithmetic and copies ran while one was open for 0% of the time, Pallas kernels for 9%

profile of v3, /device:TPU:1, one launch (start us, length us, event | category | flops | bytes accessed | tf_op | source)
XLA Modules:
  0.0 114.6 jit_solution(4330442472213337861)
XLA Ops:
  0.6 3.3 %shard_map.130 = (bf16[64,8,128]{2,1,0:T(8,128)(2,1)}, bf16[2,64,512]{2,1,0:T(8,128)(2,1)}) custom-call(s32[2,16,128]{2,1,0:T(8,128)} %bitcast.29, s32[2,128]{1,0:T(2,128)} %bitcast.34), custom_call_target="tpu_custom_call" | custom-call | tf_op jit(solution)/shard_map/pallas_call | solution.py:342
  3.9 12.0 %all-to-all-start = ((bf16[64,8,128]{2,1,0:T(8,128)(2,1)}), bf16[64,8,128]{2,1,0:T(8,128)(2,1)S(1)}, u32[]{:S(2)}, u32[]{:S(2)}) async-start(bf16[64,8,128]{2,1,0:T(8,128)(2,1)} %get-tuple-element.12), calls=%async_computation | async-start | bytes 262144 | tf_op jit(solution)/shard_map/all_to_all | solution.py:389
  15.9 0.0 copy-start.2
  15.9 1.2 %copy-done.2 = f32[512,2,256]{2,1,0:T(2,128)S(1)} copy-done((f32[512,2,256]{2,1,0:T(2,128)S(1)}, f32[512,2,256]{2,1,0:T(2,128)}, u32[]{:S(2)}) %copy-start.2) | copy-done | bytes 1048600
  17.1 0.1 shard_map.132.low_ref
  17.2 7.4 %all-to-all-done.code_ref = bf16[64,8,128]{2,1,0:T(8,128)(2,1)S(1)} async-done(((bf16[64,8,128]{2,1,0:T(8,128)(2,1)}), bf16[64,8,128]{2,1,0:T(8,128)(2,1)S(1)}, u32[]{:S(2)}, u32[]{:S(2)}) %all-to-all-start) | async-done | bytes 131104 | tf_op jit(solution)/shard_map/all_to_all | solution.py:389
  24.7 2.5 %shard_map.133 = bf16[64,64,256]{2,1,0:T(8,128)(2,1)} custom-call(bf16[64,8,128]{2,1,0:T(8,128)(2,1)S(1)} %all-to-all-done.code_ref, bf16[2,512,256]{2,1,0:T(8,128)(2,1)S(1)} %shard_map.132.low_ref), custom_call_target="tpu_custom_call" | custom-call | tf_op jit(solution)/shard_map/pallas_call | solution.py:342
  27.2 0.0 copy-start.11
  27.3 0.0 copy-start.4
  27.3 0.0 copy-start.6
  27.3 0.0 copy-start.7
  27.3 0.0 copy-start.9
  27.3 0.0 copy-start
  27.3 0.0 copy-start.5
  27.3 0.0 copy-start.10
  27.3 5.7 %all-to-all-start.1 = ((bf16[64,64,256]{2,1,0:T(8,128)(2,1)}), bf16[64,64,256]{2,1,0:T(8,128)(2,1)}, u32[]{:S(2)}, u32[]{:S(2)}) async-start(bf16[64,64,256]{2,1,0:T(8,128)(2,1)} %shard_map.133), calls=%async_computation.1 | async-start | bytes 4194304 | tf_op jit(solution)/shard_map/all_to_all | solution.py:410
  33.1 0.0 copy-done.11
  33.1 0.0 copy-done.4
  33.1 0.0 copy-done.6
  33.1 0.0 copy-done.7
  33.1 0.0 copy-done.9
  33.1 6.0 %shard_map.131.ct_ref = bf16[2,2048,128]{2,1,0:T(8,128)(2,1)S(1)} custom-call(s32[2,16,128]{2,1,0:T(8,128)S(1)} %bitcast.30, s32[2,128]{1,0:T(2,128)S(1)} %bitcast.35, bf16[2,16,128]{2,1,0:T(8,128)(2,1)S(1)} %bitcast.32, bf16[2,64,512]{2,1,0:T(8,128)(2,1)S(1)} %copy-done.4), custom_call_target="tpu_custom_call" | custom-call | tf_op jit(solution)/shard_map/pallas_call | solution.py:342
  39.2 21.3 %all-to-all-done.1.got_hbm = bf16[64,64,256]{2,1,0:T(8,128)(2,1)} async-done(((bf16[64,64,256]{2,1,0:T(8,128)(2,1)}), bf16[64,64,256]{2,1,0:T(8,128)(2,1)}, u32[]{:S(2)}, u32[]{:S(2)}) %all-to-all-start.1) | async-done | bytes 2097184 | tf_op jit(solution)/shard_map/all_to_all | solution.py:410
  60.5 0.0 copy-done
  60.5 0.0 copy-done.5
  60.5 0.0 copy-done.10
  60.5 9.0 %shard_map.134 = bf16[64,64,256]{2,1,0:T(8,128)(2,1)} custom-call(bf16[2,2048,128]{2,1,0:T(8,128)(2,1)S(1)} %shard_map.131.ct_ref, bf16[128,256]{1,0:T(8,128)(2,1)S(1)} %copy-done.5, s32[1,128]{1,0:T(1,128)S(1)} %bitcast.36, f32[1,4096]{1,0:T(1,128)S(1)} %bitcast.31, bf16[64,64,256]{2,1,0:T(8,128)(2,1)} %all-to-all-done.1.got_hbm, ...), custom_call_target="tpu_custom_call" | custom-call | tf_op jit(solution)/shard_map/pallas_call | solution.py:342
  69.5 0.0 copy-start.8
  69.5 6.5 %all-to-all-start.2 = ((bf16[64,64,256]{2,1,0:T(8,128)(2,1)}), bf16[64,64,256]{2,1,0:T(8,128)(2,1)S(1)}, u32[]{:S(2)}, u32[]{:S(2)}) async-start(bf16[64,64,256]{2,1,0:T(8,128)(2,1)} %shard_map.134), calls=%async_computation.2 | async-start | bytes 4194304 | tf_op jit(solution)/shard_map/all_to_all | solution.py:446
  76.1 0.0 copy-done.8
  76.1 3.0 %shard_map.135 = (f8e4m3fn[512,2048]{1,0:T(32,128)(4,1)S(1)}, f8e4m3fn[512,2048]{1,0:T(32,128)(4,1)}, f32[128,128]{1,0:T(8,128)S(1)}) custom-call(bf16[64,8,128]{2,1,0:T(8,128)(2,1)S(1)} %all-to-all-done.code_ref, f32[2,512]{1,0:T(2,128)S(1)} %bitcast.33), custom_call_target="tpu_custom_call" | custom-call | tf_op jit(solution)/shard_map/pallas_call | solution.py:342
  79.1 24.6 %all-to-all-done.2.share_ref = bf16[64,64,256]{2,1,0:T(8,128)(2,1)S(1)} async-done(((bf16[64,64,256]{2,1,0:T(8,128)(2,1)}), bf16[64,64,256]{2,1,0:T(8,128)(2,1)S(1)}, u32[]{:S(2)}, u32[]{:S(2)}) %all-to-all-start.2) | async-done | bytes 2097184 | tf_op jit(solution)/shard_map/all_to_all | solution.py:446
  103.7 0.0 copy-start.3
  103.7 1.2 %copy-done.3 = f8e4m3fn[512,2048]{1,0:T(32,128)(4,1)S(1)} copy-done((f8e4m3fn[512,2048]{1,0:T(32,128)(4,1)S(1)}, f8e4m3fn[512,2048]{1,0:T(32,128)(4,1)}, u32[]{:S(2)}) %copy-start.3) | copy-done | bytes 1048600
  104.9 1.0 shard_map.137.refs_1_
  105.9 0.0 copy-start.1
  105.9 3.4 %collective-permute-start.1 = (f32[640,256]{1,0:T(8,128)S(1)}, f32[640,256]{1,0:T(8,128)S(1)}, u32[]{:S(2)}, u32[]{:S(2)}) collective-permute-start(f32[640,256]{1,0:T(8,128)S(1)} %shard_map.137.refs_1_), channel_id=1, source_target_pairs={{0,64},{64,0},{1,65},{65,1},{2,66},{66,2},{3,67},{67,3},{4,68},{68... | collective-permute-start | bytes 1966088 | tf_op jit(solution)/shard_map/ppermute | solution.py:469
  109.3 1.0 shard_map.136.refs_0_
  110.4 0.1 collective-permute-start
  110.4 0.6 collective-permute-done.1.refs_3_
  111.1 1.5 %collective-permute-done.refs_2_ = f32[640,256]{1,0:T(8,128)S(1)} collective-permute-done((f32[640,256]{1,0:T(8,128)S(1)}, f32[640,256]{1,0:T(8,128)S(1)}, u32[]{:S(2)}, u32[]{:S(2)}) %collective-permute-start) | collective-permute-done | bytes 655392 | tf_op jit(solution)/shard_map/ppermute | solution.py:469
  112.5 0.0 copy-done.1
  112.5 2.0 %shard_map.138 = (f32[2048,128]{1,0:T(8,128)}, f32[2,512]{1,0:T(2,128)}, f32[2048,128]{1,0:T(8,128)}) custom-call(f32[640,256]{1,0:T(8,128)S(1)} %shard_map.136.refs_0_, f32[640,256]{1,0:T(8,128)S(1)} %shard_map.137.refs_1_, f32[640,256]{1,0:T(8,128)S(1)} %collective-permute-done.refs_2_, f32[640,256]{1,0:T(8,128)S(1)} %collective-permute-done.1.refs_3_, ...), custom_call_target="tpu_custom_call" | custom-call | tf_op jit(solution)/shard_map/pallas_call | solution.py:342
  (1 shorter events, 0.0 us)
Async XLA Ops:
  3.9 20.8 %all-to-all-start = ((bf16[64,8,128]{2,1,0:T(8,128)(2,1)}), bf16[64,8,128]{2,1,0:T(8,128)(2,1)S(1)}, u32[]{:S(2)}, u32[]{:S(2)}) async-start(bf16[64,8,128]{2,1,0:T(8,128)(2,1)} %get-tuple-element.12), calls=%async_computation | async-start | bytes 262144 | tf_op jit(solution)/shard_map/all_to_all | solution.py:389
  15.9 1.2 %copy-start.2 = (f32[512,2,256]{2,1,0:T(2,128)S(1)}, f32[512,2,256]{2,1,0:T(2,128)}, u32[]{:S(2)}) copy-start(f32[512,2,256]{2,1,0:T(2,128)} %param.16) | copy-start | bytes 3145732
  27.2 5.8 %copy-start.11 = (bf16[4096]{0:T(1024)(128)(2,1)S(1)}, bf16[4096]{0:T(1024)(128)(2,1)}, u32[]{:S(2)}) copy-start(bf16[4096]{0:T(1024)(128)(2,1)} %param.21) | copy-start | bytes 24580
  27.3 5.8 %copy-start.4 = (bf16[2,64,512]{2,1,0:T(8,128)(2,1)S(1)}, bf16[2,64,512]{2,1,0:T(8,128)(2,1)}, u32[]{:S(2)}) copy-start(bf16[2,64,512]{2,1,0:T(8,128)(2,1)} %get-tuple-element.13.rank_ref) | copy-start | bytes 393220
  27.3 5.8 %copy-start.6 = (s32[128,2,16]{0,2,1:T(8,128)S(1)}, s32[128,2,16]{0,2,1:T(8,128)}, u32[]{:S(2)}) copy-start(s32[128,2,16]{0,2,1:T(8,128)} %param.12) | copy-start | bytes 49156
  27.3 5.8 %copy-start.7 = (bf16[128,2,16]{0,2,1:T(8,128)(2,1)S(1)}, bf16[128,2,16]{0,2,1:T(8,128)(2,1)}, u32[]{:S(2)}) copy-start(bf16[128,2,16]{0,2,1:T(8,128)(2,1)} %param.14) | copy-start | bytes 24580
  27.3 5.8 %copy-start.9 = (s32[128,2]{0,1:T(2,128)S(1)}, s32[128,2]{0,1:T(2,128)}, u32[]{:S(2)}) copy-start(s32[128,2]{0,1:T(2,128)} %param.13) | copy-start | bytes 3076
  27.3 33.2 %copy-start = (bf16[768,768]{1,0:T(8,128)(2,1)S(1)}, bf16[768,768]{1,0:T(8,128)(2,1)}, u32[]{:S(2)}) copy-start(bf16[768,768]{1,0:T(8,128)(2,1)} %cross_hbm.1) | copy-start | bytes 3538948
  27.3 33.2 %copy-start.5 = (bf16[128,256]{1,0:T(8,128)(2,1)S(1)}, bf16[128,256]{1,0:T(8,128)(2,1)}, u32[]{:S(2)}) copy-start(bf16[128,256]{1,0:T(8,128)(2,1)} %dense_ref.1) | copy-start | bytes 196612
  27.3 33.1 %copy-start.10 = (s32[128]{0:T(128)S(1)}, s32[128]{0:T(128)}, u32[]{:S(2)}) copy-start(s32[128]{0:T(128)} %param.15) | copy-start | bytes 1540
  27.3 33.1 %all-to-all-start.1 = ((bf16[64,64,256]{2,1,0:T(8,128)(2,1)}), bf16[64,64,256]{2,1,0:T(8,128)(2,1)}, u32[]{:S(2)}, u32[]{:S(2)}) async-start(bf16[64,64,256]{2,1,0:T(8,128)(2,1)} %shard_map.133), calls=%async_computation.1 | async-start | bytes 4194304 | tf_op jit(solution)/shard_map/all_to_all | solution.py:410
  69.5 6.6 %copy-start.8 = (f32[512,2]{0,1:T(2,128)S(1)}, f32[512,2]{0,1:T(2,128)}, u32[]{:S(2)}) copy-start(f32[512,2]{0,1:T(2,128)} %param.18) | copy-start | bytes 12292
  69.5 34.2 %all-to-all-start.2 = ((bf16[64,64,256]{2,1,0:T(8,128)(2,1)}), bf16[64,64,256]{2,1,0:T(8,128)(2,1)S(1)}, u32[]{:S(2)}, u32[]{:S(2)}) async-start(bf16[64,64,256]{2,1,0:T(8,128)(2,1)} %shard_map.134), calls=%async_computation.2 | async-start | bytes 4194304 | tf_op jit(solution)/shard_map/all_to_all | solution.py:446
  103.7 1.2 %copy-start.3 = (f8e4m3fn[512,2048]{1,0:T(32,128)(4,1)S(1)}, f8e4m3fn[512,2048]{1,0:T(32,128)(4,1)}, u32[]{:S(2)}) copy-start(f8e4m3fn[512,2048]{1,0:T(32,128)(4,1)} %get-tuple-element.17.hot_ref) | copy-start | bytes 3145732
  105.9 6.6 %copy-start.1 = (f32[512,2,256]{2,1,0:T(2,128)S(1)}, f32[512,2,256]{2,1,0:T(2,128)}, u32[]{:S(2)}) copy-start(f32[512,2,256]{2,1,0:T(2,128)} %param.17) | copy-start | bytes 3145732
  105.9 5.1 %collective-permute-start.1 = (f32[640,256]{1,0:T(8,128)S(1)}, f32[640,256]{1,0:T(8,128)S(1)}, u32[]{:S(2)}, u32[]{:S(2)}) collective-permute-start(f32[640,256]{1,0:T(8,128)S(1)} %shard_map.137.refs_1_), channel_id=1, source_target_pairs={{0,64},{64,0},{1,65},{65,1},{2,66},{66,2},{3,67},{67,3},{4,68},{68... | collective-permute-start | bytes 1966088 | tf_op jit(solution)/shard_map/ppermute | solution.py:469
  110.4 2.2 %collective-permute-start = (f32[640,256]{1,0:T(8,128)S(1)}, f32[640,256]{1,0:T(8,128)S(1)}, u32[]{:S(2)}, u32[]{:S(2)}) collective-permute-start(f32[640,256]{1,0:T(8,128)S(1)} %shard_map.136.refs_0_), channel_id=1, source_target_pairs={{0,64},{64,0},{1,65},{65,1},{2,66},{66,2},{3,67},{67,3},{4,68},{68... | collective-permute-start | bytes 1966088 | tf_op jit(solution)/shard_map/ppermute | solution.py:469

commit v4 on v3

--- a/solution.py
+++ b/solution.py
@@ -14,7 +14,7 @@
 
 CAP = 32
 LANES = 128
-GROUP = 8
+GROUP = 32
 F32 = jnp.float32
 BF16 = jnp.bfloat16
 HOT = jnp.float8_e4m3fn
@@ -59,16 +59,27 @@
     pieces = own_rows // LANES
     before = ones_where(iota((own_rows, own_rows), 0) < iota((own_rows, own_rows), 1))
     owner_ids = iota((owners, samples), 0)
+    block = 256
+    ids = iota((samples, block), 1).astype(F32).astype(BF16)
     for t in range(tables):
         rows = rows_ref[t]
         usable = iota((slots, samples), 0) < lens_ref[t : t + 1, :]
         own = jnp.where(usable, rows >> shift, -1)
         loc = (rows & (own_rows - 1)).astype(F32)
+        columns = []
+        for n in range(own_rows // block):
+            inside = loc - n * block
+            inside = jnp.where((inside >= 0.0) & (inside < block), inside, -1.0)
+            columns.append(jnp.transpose(inside))
         for l in range(slots):
             cols = slice(l * samples, (l + 1) * samples)
             own_hot[t, :, cols] = ones_where(owner_ids == own[l : l + 1, :])
-            fill_row_hot(row_hot.at[t], l, loc[l : l + 1, :])
-        present = dot(own_hot[t], row_hot[t], NT) > 0.0
+            for n, column in enumerate(columns):
+                wanted = jnp.broadcast_to(column[:, l : l + 1], ids.shape).astype(BF16)
+                row_hot[t, cols, n * block : (n + 1) * block] = jnp.where(
+                    ids == wanted, jnp.ones_like(ids), jnp.zeros_like(ids)
+                )
+        present = dot(own_hot[t], row_hot[t]) > 0.0
         rank = dot(ones_where(present), before)
         code = jnp.where(present, rank, -1.0)
         for c in range(pieces):
@@ -380,7 +391,7 @@
         ),
         [
             pltpu.VMEM((tables, owners, slots * samples), BF16),
-            pltpu.VMEM((tables, own_rows, slots * samples), BF16),
+            pltpu.VMEM((tables, slots * samples, own_rows), BF16),
             pltpu.VMEM((owners, count, LANES), F32),
         ],
         rows,

time: 115 us -> 114 us (level)
  no operation moved by 1% of the time
where the time goes in v4:
time: 114 us
  waiting for transfers between devices  55.3 us (49%)
  starting transfers between devices  27.9 us (24%)
  Pallas kernels  27.3 us (24%)
  local copies, waits for them, and re-layouts  2.51 us (2%)
    pallas_call x9, Pallas kernels, call(): pl.pallas_call(body, out_shape=out_shape, in_specs=[hbm if n in in_hbm el...  27.3 us
    all_to_all x1, waiting for transfers between devices, local(): shares = lax.all_to_all(share, 'shard', 0, 0, tiled=True)  24.5 us
    all_to_all x1, waiting for transfers between devices, local(): got = lax.all_to_all(found, 'shard', 0, 0, tiled=True)  21.3 us
    all_to_all x1, starting transfers between devices, local(): asked = lax.all_to_all(code, 'shard', 0, 0, tiled=True)  12 us
    all_to_all x1, waiting for transfers between devices, local(): asked = lax.all_to_all(code, 'shard', 0, 0, tiled=True)  7.44 us
    all_to_all x1, starting transfers between devices, local(): shares = lax.all_to_all(share, 'shard', 0, 0, tiled=True)  6.71 us
    all_to_all x1, starting transfers between devices, local(): got = lax.all_to_all(found, 'shard', 0, 0, tiled=True)  5.71 us
    ppermute x2, starting transfers between devices, local(): peer.append(lax.ppermute(part, 'replica', [(0, 1), (1, 0)]))  3.5 us
  transfers between devices with their start and end apart: 5, of which 5 were waited for; matrix products, arithmetic and copies ran while one was open for 0% of the time, Pallas kernels for 9%

profile of v4, /device:TPU:1, one launch (start us, length us, event | category | flops | bytes accessed | tf_op | source)
XLA Modules:
  0.0 113.9 jit_solution(1839884681767244737)
XLA Ops:
  0.6 2.9 %shard_map.130 = (bf16[64,8,128]{2,1,0:T(8,128)(2,1)}, bf16[2,64,512]{2,1,0:T(8,128)(2,1)}) custom-call(s32[2,16,128]{2,1,0:T(8,128)} %bitcast.29, s32[2,128]{1,0:T(2,128)} %bitcast.34), custom_call_target="tpu_custom_call" | custom-call | tf_op jit(solution)/shard_map/pallas_call | solution.py:353
  3.5 12.0 %all-to-all-start = ((bf16[64,8,128]{2,1,0:T(8,128)(2,1)}), bf16[64,8,128]{2,1,0:T(8,128)(2,1)S(1)}, u32[]{:S(2)}, u32[]{:S(2)}) async-start(bf16[64,8,128]{2,1,0:T(8,128)(2,1)} %get-tuple-element.12), calls=%async_computation | async-start | bytes 262144 | tf_op jit(solution)/shard_map/all_to_all | solution.py:400
  15.5 0.0 copy-start.2
  15.5 1.2 %copy-done.2 = f32[512,2,256]{2,1,0:T(2,128)S(1)} copy-done((f32[512,2,256]{2,1,0:T(2,128)S(1)}, f32[512,2,256]{2,1,0:T(2,128)}, u32[]{:S(2)}) %copy-start.2) | copy-done | bytes 1048600
  16.7 0.1 shard_map.132.low_ref
  16.9 7.4 %all-to-all-done.code_ref = bf16[64,8,128]{2,1,0:T(8,128)(2,1)S(1)} async-done(((bf16[64,8,128]{2,1,0:T(8,128)(2,1)}), bf16[64,8,128]{2,1,0:T(8,128)(2,1)S(1)}, u32[]{:S(2)}, u32[]{:S(2)}) %all-to-all-start) | async-done | bytes 131104 | tf_op jit(solution)/shard_map/all_to_all | solution.py:400
  24.3 2.3 %shard_map.133 = bf16[64,64,256]{2,1,0:T(8,128)(2,1)} custom-call(bf16[64,8,128]{2,1,0:T(8,128)(2,1)S(1)} %all-to-all-done.code_ref, bf16[2,512,256]{2,1,0:T(8,128)(2,1)S(1)} %shard_map.132.low_ref), custom_call_target="tpu_custom_call" | custom-call | tf_op jit(solution)/shard_map/pallas_call | solution.py:353
  26.6 0.0 copy-start.11
  26.6 0.0 copy-start.4
  26.6 0.0 copy-start.6
  26.6 0.0 copy-start.7
  26.6 0.0 copy-start.9
  26.6 0.0 copy-start
  26.6 0.0 copy-start.5
  26.7 0.0 copy-start.10
  26.7 5.7 %all-to-all-start.1 = ((bf16[64,64,256]{2,1,0:T(8,128)(2,1)}), bf16[64,64,256]{2,1,0:T(8,128)(2,1)}, u32[]{:S(2)}, u32[]{:S(2)}) async-start(bf16[64,64,256]{2,1,0:T(8,128)(2,1)} %shard_map.133), calls=%async_computation.1 | async-start | bytes 4194304 | tf_op jit(solution)/shard_map/all_to_all | solution.py:421
  32.4 0.0 copy-done.11
  32.4 0.0 copy-done.4
  32.4 0.0 copy-done.6
  32.4 0.0 copy-done.7
  32.4 0.0 copy-done.9
  32.4 6.0 %shard_map.131.ct_ref = bf16[2,2048,128]{2,1,0:T(8,128)(2,1)S(1)} custom-call(s32[2,16,128]{2,1,0:T(8,128)S(1)} %bitcast.30, s32[2,128]{1,0:T(2,128)S(1)} %bitcast.35, bf16[2,16,128]{2,1,0:T(8,128)(2,1)S(1)} %bitcast.32, bf16[2,64,512]{2,1,0:T(8,128)(2,1)S(1)} %copy-done.4), custom_call_target="tpu_custom_call" | custom-call | tf_op jit(solution)/shard_map/pallas_call | solution.py:353
  38.5 21.3 %all-to-all-done.1.got_hbm = bf16[64,64,256]{2,1,0:T(8,128)(2,1)} async-done(((bf16[64,64,256]{2,1,0:T(8,128)(2,1)}), bf16[64,64,256]{2,1,0:T(8,128)(2,1)}, u32[]{:S(2)}, u32[]{:S(2)}) %all-to-all-start.1) | async-done | bytes 2097184 | tf_op jit(solution)/shard_map/all_to_all | solution.py:421
  59.8 0.0 copy-done
  59.8 0.0 copy-done.5
  59.8 0.0 copy-done.10
  59.8 9.0 %shard_map.134 = bf16[64,64,256]{2,1,0:T(8,128)(2,1)} custom-call(bf16[2,2048,128]{2,1,0:T(8,128)(2,1)S(1)} %shard_map.131.ct_ref, bf16[128,256]{1,0:T(8,128)(2,1)S(1)} %copy-done.5, s32[1,128]{1,0:T(1,128)S(1)} %bitcast.36, f32[1,4096]{1,0:T(1,128)S(1)} %bitcast.31, bf16[64,64,256]{2,1,0:T(8,128)(2,1)} %all-to-all-done.1.got_hbm, ...), custom_call_target="tpu_custom_call" | custom-call | tf_op jit(solution)/shard_map/pallas_call | solution.py:353
  68.8 0.0 copy-start.8
  68.8 6.7 %all-to-all-start.2 = ((bf16[64,64,256]{2,1,0:T(8,128)(2,1)}), bf16[64,64,256]{2,1,0:T(8,128)(2,1)S(1)}, u32[]{:S(2)}, u32[]{:S(2)}) async-start(bf16[64,64,256]{2,1,0:T(8,128)(2,1)} %shard_map.134), calls=%async_computation.2 | async-start | bytes 4194304 | tf_op jit(solution)/shard_map/all_to_all | solution.py:457
  75.6 0.0 copy-done.8
  75.6 3.0 %shard_map.135 = (f8e4m3fn[512,2048]{1,0:T(32,128)(4,1)S(1)}, f8e4m3fn[512,2048]{1,0:T(32,128)(4,1)}, f32[128,128]{1,0:T(8,128)S(1)}) custom-call(bf16[64,8,128]{2,1,0:T(8,128)(2,1)S(1)} %all-to-all-done.code_ref, f32[2,512]{1,0:T(2,128)S(1)} %bitcast.33), custom_call_target="tpu_custom_call" | custom-call | tf_op jit(solution)/shard_map/pallas_call | solution.py:353
  78.6 24.5 %all-to-all-done.2.share_ref = bf16[64,64,256]{2,1,0:T(8,128)(2,1)S(1)} async-done(((bf16[64,64,256]{2,1,0:T(8,128)(2,1)}), bf16[64,64,256]{2,1,0:T(8,128)(2,1)S(1)}, u32[]{:S(2)}, u32[]{:S(2)}) %all-to-all-start.2) | async-done | bytes 2097184 | tf_op jit(solution)/shard_map/all_to_all | solution.py:457
  103.0 0.0 copy-start.3
  103.0 1.2 %copy-done.3 = f8e4m3fn[512,2048]{1,0:T(32,128)(4,1)S(1)} copy-done((f8e4m3fn[512,2048]{1,0:T(32,128)(4,1)S(1)}, f8e4m3fn[512,2048]{1,0:T(32,128)(4,1)}, u32[]{:S(2)}) %copy-start.3) | copy-done | bytes 1048600
  104.3 1.0 shard_map.137.refs_1_
  105.2 0.0 copy-start.1
  105.3 3.4 %collective-permute-start.1 = (f32[640,256]{1,0:T(8,128)S(1)}, f32[640,256]{1,0:T(8,128)S(1)}, u32[]{:S(2)}, u32[]{:S(2)}) collective-permute-start(f32[640,256]{1,0:T(8,128)S(1)} %shard_map.137.refs_1_), channel_id=1, source_target_pairs={{0,64},{64,0},{1,65},{65,1},{2,66},{66,2},{3,67},{67,3},{4,68},{68... | collective-permute-start | bytes 1966088 | tf_op jit(solution)/shard_map/ppermute | solution.py:480
  108.7 1.0 shard_map.136.refs_0_
  109.7 0.1 collective-permute-start
  109.8 0.6 collective-permute-done.1.refs_3_
  110.4 1.5 %collective-permute-done.refs_2_ = f32[640,256]{1,0:T(8,128)S(1)} collective-permute-done((f32[640,256]{1,0:T(8,128)S(1)}, f32[640,256]{1,0:T(8,128)S(1)}, u32[]{:S(2)}, u32[]{:S(2)}) %collective-permute-start) | collective-permute-done | bytes 655392 | tf_op jit(solution)/shard_map/ppermute | solution.py:480
  111.8 0.0 copy-done.1
  111.8 2.0 %shard_map.138 = (f32[2048,128]{1,0:T(8,128)}, f32[2,512]{1,0:T(2,128)}, f32[2048,128]{1,0:T(8,128)}) custom-call(f32[640,256]{1,0:T(8,128)S(1)} %shard_map.136.refs_0_, f32[640,256]{1,0:T(8,128)S(1)} %shard_map.137.refs_1_, f32[640,256]{1,0:T(8,128)S(1)} %collective-permute-done.refs_2_, f32[640,256]{1,0:T(8,128)S(1)} %collective-permute-done.1.refs_3_, ...), custom_call_target="tpu_custom_call" | custom-call | tf_op jit(solution)/shard_map/pallas_call | solution.py:353
  (1 shorter events, 0.0 us)
Async XLA Ops:
  3.5 20.8 %all-to-all-start = ((bf16[64,8,128]{2,1,0:T(8,128)(2,1)}), bf16[64,8,128]{2,1,0:T(8,128)(2,1)S(1)}, u32[]{:S(2)}, u32[]{:S(2)}) async-start(bf16[64,8,128]{2,1,0:T(8,128)(2,1)} %get-tuple-element.12), calls=%async_computation | async-start | bytes 262144 | tf_op jit(solution)/shard_map/all_to_all | solution.py:400
  15.5 1.2 %copy-start.2 = (f32[512,2,256]{2,1,0:T(2,128)S(1)}, f32[512,2,256]{2,1,0:T(2,128)}, u32[]{:S(2)}) copy-start(f32[512,2,256]{2,1,0:T(2,128)} %param.16) | copy-start | bytes 3145732
  26.6 5.8 %copy-start.11 = (bf16[4096]{0:T(1024)(128)(2,1)S(1)}, bf16[4096]{0:T(1024)(128)(2,1)}, u32[]{:S(2)}) copy-start(bf16[4096]{0:T(1024)(128)(2,1)} %param.21) | copy-start | bytes 24580
  26.6 5.8 %copy-start.4 = (bf16[2,64,512]{2,1,0:T(8,128)(2,1)S(1)}, bf16[2,64,512]{2,1,0:T(8,128)(2,1)}, u32[]{:S(2)}) copy-start(bf16[2,64,512]{2,1,0:T(8,128)(2,1)} %get-tuple-element.13.rank_ref) | copy-start | bytes 393220
  26.6 5.8 %copy-start.6 = (s32[128,2,16]{0,2,1:T(8,128)S(1)}, s32[128,2,16]{0,2,1:T(8,128)}, u32[]{:S(2)}) copy-start(s32[128,2,16]{0,2,1:T(8,128)} %param.12) | copy-start | bytes 49156
  26.6 5.8 %copy-start.7 = (bf16[128,2,16]{0,2,1:T(8,128)(2,1)S(1)}, bf16[128,2,16]{0,2,1:T(8,128)(2,1)}, u32[]{:S(2)}) copy-start(bf16[128,2,16]{0,2,1:T(8,128)(2,1)} %param.14) | copy-start | bytes 24580
  26.6 5.8 %copy-start.9 = (s32[128,2]{0,1:T(2,128)S(1)}, s32[128,2]{0,1:T(2,128)}, u32[]{:S(2)}) copy-start(s32[128,2]{0,1:T(2,128)} %param.13) | copy-start | bytes 3076
  26.6 33.2 %copy-start = (bf16[768,768]{1,0:T(8,128)(2,1)S(1)}, bf16[768,768]{1,0:T(8,128)(2,1)}, u32[]{:S(2)}) copy-start(bf16[768,768]{1,0:T(8,128)(2,1)} %cross_hbm.1) | copy-start | bytes 3538948
  26.6 33.2 %copy-start.5 = (bf16[128,256]{1,0:T(8,128)(2,1)S(1)}, bf16[128,256]{1,0:T(8,128)(2,1)}, u32[]{:S(2)}) copy-start(bf16[128,256]{1,0:T(8,128)(2,1)} %dense_ref.1) | copy-start | bytes 196612
  26.7 33.1 %copy-start.10 = (s32[128]{0:T(128)S(1)}, s32[128]{0:T(128)}, u32[]{:S(2)}) copy-start(s32[128]{0:T(128)} %param.15) | copy-start | bytes 1540
  26.7 33.1 %all-to-all-start.1 = ((bf16[64,64,256]{2,1,0:T(8,128)(2,1)}), bf16[64,64,256]{2,1,0:T(8,128)(2,1)}, u32[]{:S(2)}, u32[]{:S(2)}) async-start(bf16[64,64,256]{2,1,0:T(8,128)(2,1)} %shard_map.133), calls=%async_computation.1 | async-start | bytes 4194304 | tf_op jit(solution)/shard_map/all_to_all | solution.py:421
  68.8 6.7 %copy-start.8 = (f32[512,2]{0,1:T(2,128)S(1)}, f32[512,2]{0,1:T(2,128)}, u32[]{:S(2)}) copy-start(f32[512,2]{0,1:T(2,128)} %param.18) | copy-start | bytes 12292
  68.8 34.2 %all-to-all-start.2 = ((bf16[64,64,256]{2,1,0:T(8,128)(2,1)}), bf16[64,64,256]{2,1,0:T(8,128)(2,1)S(1)}, u32[]{:S(2)}, u32[]{:S(2)}) async-start(bf16[64,64,256]{2,1,0:T(8,128)(2,1)} %shard_map.134), calls=%async_computation.2 | async-start | bytes 4194304 | tf_op jit(solution)/shard_map/all_to_all | solution.py:457
  103.0 1.2 %copy-start.3 = (f8e4m3fn[512,2048]{1,0:T(32,128)(4,1)S(1)}, f8e4m3fn[512,2048]{1,0:T(32,128)(4,1)}, u32[]{:S(2)}) copy-start(f8e4m3fn[512,2048]{1,0:T(32,128)(4,1)} %get-tuple-element.17.hot_ref) | copy-start | bytes 3145732
  105.2 6.6 %copy-start.1 = (f32[512,2,256]{2,1,0:T(2,128)S(1)}, f32[512,2,256]{2,1,0:T(2,128)}, u32[]{:S(2)}) copy-start(f32[512,2,256]{2,1,0:T(2,128)} %param.17) | copy-start | bytes 3145732
  105.3 5.1 %collective-permute-start.1 = (f32[640,256]{1,0:T(8,128)S(1)}, f32[640,256]{1,0:T(8,128)S(1)}, u32[]{:S(2)}, u32[]{:S(2)}) collective-permute-start(f32[640,256]{1,0:T(8,128)S(1)} %shard_map.137.refs_1_), channel_id=1, source_target_pairs={{0,64},{64,0},{1,65},{65,1},{2,66},{66,2},{3,67},{67,3},{4,68},{68... | collective-permute-start | bytes 1966088 | tf_op jit(solution)/shard_map/ppermute | solution.py:480
  109.7 2.2 %collective-permute-start = (f32[640,256]{1,0:T(8,128)S(1)}, f32[640,256]{1,0:T(8,128)S(1)}, u32[]{:S(2)}, u32[]{:S(2)}) collective-permute-start(f32[640,256]{1,0:T(8,128)S(1)} %shard_map.136.refs_0_), channel_id=1, source_target_pairs={{0,64},{64,0},{1,65},{65,1},{2,66},{66,2},{3,67},{67,3},{4,68},{68... | collective-permute-start | bytes 1966088 | tf_op jit(solution)/shard_map/ppermute | solution.py:480

commit v5 on v4

--- a/solution.py
+++ b/solution.py
@@ -298,8 +298,9 @@
         stats = jnp.where(lane_ids == pieces + c, scale, stats)
         stats = jnp.where(lane_ids == 2 * pieces + c, decay, stats)
         out_ref[c * LANES : (c + 1) * LANES, :] = (1.0 - beta_first) * grad
-    out_ref[own_rows:, :LANES] = stats
-    out_ref[own_rows:, LANES:] = jnp.zeros((LANES, width - LANES), F32)
+    half = LANES // 2
+    out_ref[own_rows:, :LANES] = stats[:half, :]
+    out_ref[own_rows:, LANES:] = stats[half:, :]
 
 
 def adam_kernel(tables, *refs):
@@ -311,7 +312,10 @@
     halves = width // LANES
     for t in range(tables):
         pair = (mine_refs[t], peer_refs[t])
-        stats = [ref[own_rows:, :LANES] for ref in pair]
+        stats = [
+            jnp.concatenate([ref[own_rows:, :LANES], ref[own_rows:, LANES:]], axis=0)
+            for ref in pair
+        ]
         second = jnp.transpose((stats[0] + stats[1]) * 0.5)
         for c in range(pieces):
             rows = slice(c * LANES, (c + 1) * LANES)
@@ -470,7 +474,7 @@
         part = call(
             functools.partial(collect_kernel, t, tables),
             14,
-            shape((own_rows + LANES, width), F32),
+            shape((own_rows + LANES // 2, width), F32),
             [],
             hots[t],
             columns,

time: 114 us -> 114 us (level)
  no operation moved by 1% of the time
where the time goes in v5:
time: 114 us
  waiting for transfers between devices  55.2 us (48%)
  starting transfers between devices  27.9 us (24%)
  Pallas kernels  27.3 us (24%)
  local copies, waits for them, and re-layouts  2.51 us (2%)
    pallas_call x9, Pallas kernels, call(): pl.pallas_call(body, out_shape=out_shape, in_specs=[hbm if n in in_hbm el...  27.3 us
    all_to_all x1, waiting for transfers between devices, local(): shares = lax.all_to_all(share, 'shard', 0, 0, tiled=True)  24.5 us
    all_to_all x1, waiting for transfers between devices, local(): got = lax.all_to_all(found, 'shard', 0, 0, tiled=True)  21.3 us
    all_to_all x1, starting transfers between devices, local(): asked = lax.all_to_all(code, 'shard', 0, 0, tiled=True)  12 us
    all_to_all x1, waiting for transfers between devices, local(): asked = lax.all_to_all(code, 'shard', 0, 0, tiled=True)  7.44 us
    all_to_all x1, starting transfers between devices, local(): shares = lax.all_to_all(share, 'shard', 0, 0, tiled=True)  6.71 us
    all_to_all x1, starting transfers between devices, local(): got = lax.all_to_all(found, 'shard', 0, 0, tiled=True)  5.71 us
    ppermute x2, starting transfers between devices, local(): peer.append(lax.ppermute(part, 'replica', [(0, 1), (1, 0)]))  3.5 us
  transfers between devices with their start and end apart: 5, of which 5 were waited for; matrix products, arithmetic and copies ran while one was open for 0% of the time, Pallas kernels for 9%

profile of v5, /device:TPU:1, one launch (start us, length us, event | category | flops | bytes accessed | tf_op | source)
XLA Modules:
  0.0 113.8 jit_solution(1350660236345059593)
XLA Ops:
  0.6 2.9 %shard_map.130 = (bf16[64,8,128]{2,1,0:T(8,128)(2,1)}, bf16[2,64,512]{2,1,0:T(8,128)(2,1)}) custom-call(s32[2,16,128]{2,1,0:T(8,128)} %bitcast.29, s32[2,128]{1,0:T(2,128)} %bitcast.34), custom_call_target="tpu_custom_call" | custom-call | tf_op jit(solution)/shard_map/pallas_call | solution.py:357
  3.5 12.0 %all-to-all-start = ((bf16[64,8,128]{2,1,0:T(8,128)(2,1)}), bf16[64,8,128]{2,1,0:T(8,128)(2,1)S(1)}, u32[]{:S(2)}, u32[]{:S(2)}) async-start(bf16[64,8,128]{2,1,0:T(8,128)(2,1)} %get-tuple-element.12), calls=%async_computation | async-start | bytes 262144 | tf_op jit(solution)/shard_map/all_to_all | solution.py:404
  15.5 0.0 copy-start.1
  15.5 1.2 %copy-done.1 = f32[512,2,256]{2,1,0:T(2,128)S(1)} copy-done((f32[512,2,256]{2,1,0:T(2,128)S(1)}, f32[512,2,256]{2,1,0:T(2,128)}, u32[]{:S(2)}) %copy-start.1) | copy-done | bytes 1048600
  16.7 0.1 shard_map.132.low_ref
  16.9 7.4 %all-to-all-done.code_ref = bf16[64,8,128]{2,1,0:T(8,128)(2,1)S(1)} async-done(((bf16[64,8,128]{2,1,0:T(8,128)(2,1)}), bf16[64,8,128]{2,1,0:T(8,128)(2,1)S(1)}, u32[]{:S(2)}, u32[]{:S(2)}) %all-to-all-start) | async-done | bytes 131104 | tf_op jit(solution)/shard_map/all_to_all | solution.py:404
  24.3 2.3 %shard_map.133 = bf16[64,64,256]{2,1,0:T(8,128)(2,1)} custom-call(bf16[64,8,128]{2,1,0:T(8,128)(2,1)S(1)} %all-to-all-done.code_ref, bf16[2,512,256]{2,1,0:T(8,128)(2,1)S(1)} %shard_map.132.low_ref), custom_call_target="tpu_custom_call" | custom-call | tf_op jit(solution)/shard_map/pallas_call | solution.py:357
  26.6 0.0 copy-start.11
  26.6 0.0 copy-start.4
  26.6 0.0 copy-start.6
  26.6 0.0 copy-start.7
  26.6 0.0 copy-start.9
  26.6 0.0 copy-start
  26.6 0.0 copy-start.5
  26.7 0.0 copy-start.10
  26.7 5.7 %all-to-all-start.1 = ((bf16[64,64,256]{2,1,0:T(8,128)(2,1)}), bf16[64,64,256]{2,1,0:T(8,128)(2,1)}, u32[]{:S(2)}, u32[]{:S(2)}) async-start(bf16[64,64,256]{2,1,0:T(8,128)(2,1)} %shard_map.133), calls=%async_computation.1 | async-start | bytes 4194304 | tf_op jit(solution)/shard_map/all_to_all | solution.py:425
  32.4 0.0 copy-done.11
  32.4 0.0 copy-done.4
  32.4 0.0 copy-done.6
  32.4 0.0 copy-done.7
  32.4 0.0 copy-done.9
  32.4 6.0 %shard_map.131.ct_ref = bf16[2,2048,128]{2,1,0:T(8,128)(2,1)S(1)} custom-call(s32[2,16,128]{2,1,0:T(8,128)S(1)} %bitcast.30, s32[2,128]{1,0:T(2,128)S(1)} %bitcast.35, bf16[2,16,128]{2,1,0:T(8,128)(2,1)S(1)} %bitcast.32, bf16[2,64,512]{2,1,0:T(8,128)(2,1)S(1)} %copy-done.4), custom_call_target="tpu_custom_call" | custom-call | tf_op jit(solution)/shard_map/pallas_call | solution.py:357
  38.5 21.3 %all-to-all-done.1.got_hbm = bf16[64,64,256]{2,1,0:T(8,128)(2,1)} async-done(((bf16[64,64,256]{2,1,0:T(8,128)(2,1)}), bf16[64,64,256]{2,1,0:T(8,128)(2,1)}, u32[]{:S(2)}, u32[]{:S(2)}) %all-to-all-start.1) | async-done | bytes 2097184 | tf_op jit(solution)/shard_map/all_to_all | solution.py:425
  59.8 0.0 copy-done
  59.8 0.0 copy-done.5
  59.8 0.0 copy-done.10
  59.8 9.0 %shard_map.134 = bf16[64,64,256]{2,1,0:T(8,128)(2,1)} custom-call(bf16[2,2048,128]{2,1,0:T(8,128)(2,1)S(1)} %shard_map.131.ct_ref, bf16[128,256]{1,0:T(8,128)(2,1)S(1)} %copy-done.5, s32[1,128]{1,0:T(1,128)S(1)} %bitcast.36, f32[1,4096]{1,0:T(1,128)S(1)} %bitcast.31, bf16[64,64,256]{2,1,0:T(8,128)(2,1)} %all-to-all-done.1.got_hbm, ...), custom_call_target="tpu_custom_call" | custom-call | tf_op jit(solution)/shard_map/pallas_call | solution.py:357
  68.8 0.0 copy-start.8
  68.8 6.7 %all-to-all-start.2 = ((bf16[64,64,256]{2,1,0:T(8,128)(2,1)}), bf16[64,64,256]{2,1,0:T(8,128)(2,1)S(1)}, u32[]{:S(2)}, u32[]{:S(2)}) async-start(bf16[64,64,256]{2,1,0:T(8,128)(2,1)} %shard_map.134), calls=%async_computation.2 | async-start | bytes 4194304 | tf_op jit(solution)/shard_map/all_to_all | solution.py:461
  75.6 0.0 copy-done.8
  75.6 3.0 %shard_map.135 = (f8e4m3fn[512,2048]{1,0:T(32,128)(4,1)S(1)}, f8e4m3fn[512,2048]{1,0:T(32,128)(4,1)}, f32[128,128]{1,0:T(8,128)S(1)}) custom-call(bf16[64,8,128]{2,1,0:T(8,128)(2,1)S(1)} %all-to-all-done.code_ref, f32[2,512]{1,0:T(2,128)S(1)} %bitcast.33), custom_call_target="tpu_custom_call" | custom-call | tf_op jit(solution)/shard_map/pallas_call | solution.py:357
  78.6 24.5 %all-to-all-done.2.share_ref = bf16[64,64,256]{2,1,0:T(8,128)(2,1)S(1)} async-done(((bf16[64,64,256]{2,1,0:T(8,128)(2,1)}), bf16[64,64,256]{2,1,0:T(8,128)(2,1)S(1)}, u32[]{:S(2)}, u32[]{:S(2)}) %all-to-all-start.2) | async-done | bytes 2097184 | tf_op jit(solution)/shard_map/all_to_all | solution.py:461
  103.0 0.0 copy-start.3
  103.0 1.2 %copy-done.3 = f8e4m3fn[512,2048]{1,0:T(32,128)(4,1)S(1)} copy-done((f8e4m3fn[512,2048]{1,0:T(32,128)(4,1)S(1)}, f8e4m3fn[512,2048]{1,0:T(32,128)(4,1)}, u32[]{:S(2)}) %copy-start.3) | copy-done | bytes 1048600
  104.3 1.0 shard_map.137.refs_1_
  105.2 0.0 copy-start.2
  105.3 3.4 %collective-permute-start.1 = (f32[576,256]{1,0:T(8,128)S(1)}, f32[576,256]{1,0:T(8,128)S(1)}, u32[]{:S(2)}, u32[]{:S(2)}) collective-permute-start(f32[576,256]{1,0:T(8,128)S(1)} %shard_map.137.refs_1_), channel_id=1, source_target_pairs={{0,64},{64,0},{1,65},{65,1},{2,66},{66,2},{3,67},{67,3},{4,68},{68... | collective-permute-start | bytes 1769480 | tf_op jit(solution)/shard_map/ppermute | solution.py:484
  108.7 1.0 shard_map.136.refs_0_
  109.7 0.1 collective-permute-start
  109.8 0.5 collective-permute-done.1.refs_3_
  110.3 1.5 %collective-permute-done.refs_2_ = f32[576,256]{1,0:T(8,128)S(1)} collective-permute-done((f32[576,256]{1,0:T(8,128)S(1)}, f32[576,256]{1,0:T(8,128)S(1)}, u32[]{:S(2)}, u32[]{:S(2)}) %collective-permute-start) | collective-permute-done | bytes 589856 | tf_op jit(solution)/shard_map/ppermute | solution.py:484
  111.7 0.0 copy-done.2
  111.7 2.0 %shard_map.138 = (f32[2048,128]{1,0:T(8,128)}, f32[2,512]{1,0:T(2,128)}, f32[2048,128]{1,0:T(8,128)}) custom-call(f32[576,256]{1,0:T(8,128)S(1)} %shard_map.136.refs_0_, f32[576,256]{1,0:T(8,128)S(1)} %shard_map.137.refs_1_, f32[576,256]{1,0:T(8,128)S(1)} %collective-permute-done.refs_2_, f32[576,256]{1,0:T(8,128)S(1)} %collective-permute-done.1.refs_3_, ...), custom_call_target="tpu_custom_call" | custom-call | tf_op jit(solution)/shard_map/pallas_call | solution.py:357
  (1 shorter events, 0.0 us)
Async XLA Ops:
  3.5 20.8 %all-to-all-start = ((bf16[64,8,128]{2,1,0:T(8,128)(2,1)}), bf16[64,8,128]{2,1,0:T(8,128)(2,1)S(1)}, u32[]{:S(2)}, u32[]{:S(2)}) async-start(bf16[64,8,128]{2,1,0:T(8,128)(2,1)} %get-tuple-element.12), calls=%async_computation | async-start | bytes 262144 | tf_op jit(solution)/shard_map/all_to_all | solution.py:404
  15.5 1.2 %copy-start.1 = (f32[512,2,256]{2,1,0:T(2,128)S(1)}, f32[512,2,256]{2,1,0:T(2,128)}, u32[]{:S(2)}) copy-start(f32[512,2,256]{2,1,0:T(2,128)} %param.16) | copy-start | bytes 3145732
  26.6 5.8 %copy-start.11 = (bf16[4096]{0:T(1024)(128)(2,1)S(1)}, bf16[4096]{0:T(1024)(128)(2,1)}, u32[]{:S(2)}) copy-start(bf16[4096]{0:T(1024)(128)(2,1)} %param.21) | copy-start | bytes 24580
  26.6 5.8 %copy-start.4 = (bf16[2,64,512]{2,1,0:T(8,128)(2,1)S(1)}, bf16[2,64,512]{2,1,0:T(8,128)(2,1)}, u32[]{:S(2)}) copy-start(bf16[2,64,512]{2,1,0:T(8,128)(2,1)} %get-tuple-element.13.rank_ref) | copy-start | bytes 393220
  26.6 5.8 %copy-start.6 = (s32[128,2,16]{0,2,1:T(8,128)S(1)}, s32[128,2,16]{0,2,1:T(8,128)}, u32[]{:S(2)}) copy-start(s32[128,2,16]{0,2,1:T(8,128)} %param.12) | copy-start | bytes 49156
  26.6 5.8 %copy-start.7 = (bf16[128,2,16]{0,2,1:T(8,128)(2,1)S(1)}, bf16[128,2,16]{0,2,1:T(8,128)(2,1)}, u32[]{:S(2)}) copy-start(bf16[128,2,16]{0,2,1:T(8,128)(2,1)} %param.14) | copy-start | bytes 24580
  26.6 5.8 %copy-start.9 = (s32[128,2]{0,1:T(2,128)S(1)}, s32[128,2]{0,1:T(2,128)}, u32[]{:S(2)}) copy-start(s32[128,2]{0,1:T(2,128)} %param.13) | copy-start | bytes 3076
  26.6 33.2 %copy-start = (bf16[768,768]{1,0:T(8,128)(2,1)S(1)}, bf16[768,768]{1,0:T(8,128)(2,1)}, u32[]{:S(2)}) copy-start(bf16[768,768]{1,0:T(8,128)(2,1)} %cross_hbm.1) | copy-start | bytes 3538948
  26.6 33.2 %copy-start.5 = (bf16[128,256]{1,0:T(8,128)(2,1)S(1)}, bf16[128,256]{1,0:T(8,128)(2,1)}, u32[]{:S(2)}) copy-start(bf16[128,256]{1,0:T(8,128)(2,1)} %dense_ref.1) | copy-start | bytes 196612
  26.7 33.1 %copy-start.10 = (s32[128]{0:T(128)S(1)}, s32[128]{0:T(128)}, u32[]{:S(2)}) copy-start(s32[128]{0:T(128)} %param.15) | copy-start | bytes 1540
  26.7 33.1 %all-to-all-start.1 = ((bf16[64,64,256]{2,1,0:T(8,128)(2,1)}), bf16[64,64,256]{2,1,0:T(8,128)(2,1)}, u32[]{:S(2)}, u32[]{:S(2)}) async-start(bf16[64,64,256]{2,1,0:T(8,128)(2,1)} %shard_map.133), calls=%async_computation.1 | async-start | bytes 4194304 | tf_op jit(solution)/shard_map/all_to_all | solution.py:425
  68.8 6.7 %copy-start.8 = (f32[512,2]{0,1:T(2,128)S(1)}, f32[512,2]{0,1:T(2,128)}, u32[]{:S(2)}) copy-start(f32[512,2]{0,1:T(2,128)} %param.18) | copy-start | bytes 12292
  68.8 34.2 %all-to-all-start.2 = ((bf16[64,64,256]{2,1,0:T(8,128)(2,1)}), bf16[64,64,256]{2,1,0:T(8,128)(2,1)S(1)}, u32[]{:S(2)}, u32[]{:S(2)}) async-start(bf16[64,64,256]{2,1,0:T(8,128)(2,1)} %shard_map.134), calls=%async_computation.2 | async-start | bytes 4194304 | tf_op jit(solution)/shard_map/all_to_all | solution.py:461
  103.0 1.2 %copy-start.3 = (f8e4m3fn[512,2048]{1,0:T(32,128)(4,1)S(1)}, f8e4m3fn[512,2048]{1,0:T(32,128)(4,1)}, u32[]{:S(2)}) copy-start(f8e4m3fn[512,2048]{1,0:T(32,128)(4,1)} %get-tuple-element.17.hot_ref) | copy-start | bytes 3145732
  105.2 6.5 %copy-start.2 = (f32[512,2,256]{2,1,0:T(2,128)S(1)}, f32[512,2,256]{2,1,0:T(2,128)}, u32[]{:S(2)}) copy-start(f32[512,2,256]{2,1,0:T(2,128)} %param.17) | copy-start | bytes 3145732
  105.3 5.0 %collective-permute-start.1 = (f32[576,256]{1,0:T(8,128)S(1)}, f32[576,256]{1,0:T(8,128)S(1)}, u32[]{:S(2)}, u32[]{:S(2)}) collective-permute-start(f32[576,256]{1,0:T(8,128)S(1)} %shard_map.137.refs_1_), channel_id=1, source_target_pairs={{0,64},{64,0},{1,65},{65,1},{2,66},{66,2},{3,67},{67,3},{4,68},{68... | collective-permute-start | bytes 1769480 | tf_op jit(solution)/shard_map/ppermute | solution.py:484
  109.7 2.1 %collective-permute-start = (f32[576,256]{1,0:T(8,128)S(1)}, f32[576,256]{1,0:T(8,128)S(1)}, u32[]{:S(2)}, u32[]{:S(2)}) collective-permute-start(f32[576,256]{1,0:T(8,128)S(1)} %shard_map.136.refs_0_), channel_id=1, source_target_pairs={{0,64},{64,0},{1,65},{65,1},{2,66},{66,2},{3,67},{67,3},{4,68},{68... | collective-permute-start | bytes 1769480 | tf_op jit(solution)/shard_map/ppermute | solution.py:484

commit v6 on v4

--- a/solution.py
+++ b/solution.py
@@ -58,13 +58,13 @@
     shift = own_rows.bit_length() - 1
     pieces = own_rows // LANES
     before = ones_where(iota((own_rows, own_rows), 0) < iota((own_rows, own_rows), 1))
-    owner_ids = iota((owners, samples), 0)
+    owner_ids = iota((owners, samples), 0).astype(F32).astype(BF16)
     block = 256
     ids = iota((samples, block), 1).astype(F32).astype(BF16)
     for t in range(tables):
         rows = rows_ref[t]
         usable = iota((slots, samples), 0) < lens_ref[t : t + 1, :]
-        own = jnp.where(usable, rows >> shift, -1)
+        own = jnp.where(usable, rows >> shift, -1).astype(F32)
         loc = (rows & (own_rows - 1)).astype(F32)
         columns = []
         for n in range(own_rows // block):
@@ -73,7 +73,7 @@
             columns.append(jnp.transpose(inside))
         for l in range(slots):
             cols = slice(l * samples, (l + 1) * samples)
-            own_hot[t, :, cols] = ones_where(owner_ids == own[l : l + 1, :])
+            own_hot[t, :, cols] = matches(owner_ids, own[l : l + 1, :])
             for n, column in enumerate(columns):
                 wanted = jnp.broadcast_to(column[:, l : l + 1], ids.shape).astype(BF16)
                 row_hot[t, cols, n * block : (n + 1) * block] = jnp.where(

time: 114 us -> 114 us (level)
  no operation moved by 1% of the time
where the time goes in v6:
time: 114 us
  waiting for transfers between devices  55.3 us (49%)
  starting transfers between devices  27.9 us (24%)
  Pallas kernels  27.3 us (24%)
  local copies, waits for them, and re-layouts  2.51 us (2%)
    pallas_call x9, Pallas kernels, call(): pl.pallas_call(body, out_shape=out_shape, in_specs=[hbm if n in in_hbm el...  27.3 us
    all_to_all x1, waiting for transfers between devices, local(): shares = lax.all_to_all(share, 'shard', 0, 0, tiled=True)  24.5 us
    all_to_all x1, waiting for transfers between devices, local(): got = lax.all_to_all(found, 'shard', 0, 0, tiled=True)  21.3 us
    all_to_all x1, starting transfers between devices, local(): asked = lax.all_to_all(code, 'shard', 0, 0, tiled=True)  12 us
    all_to_all x1, waiting for transfers between devices, local(): asked = lax.all_to_all(code, 'shard', 0, 0, tiled=True)  7.44 us
    all_to_all x1, starting transfers between devices, local(): shares = lax.all_to_all(share, 'shard', 0, 0, tiled=True)  6.71 us
    all_to_all x1, starting transfers between devices, local(): got = lax.all_to_all(found, 'shard', 0, 0, tiled=True)  5.71 us
    ppermute x2, starting transfers between devices, local(): peer.append(lax.ppermute(part, 'replica', [(0, 1), (1, 0)]))  3.5 us
  transfers between devices with their start and end apart: 5, of which 5 were waited for; matrix products, arithmetic and copies ran while one was open for 0% of the time, Pallas kernels for 9%

profile of v6, /device:TPU:1, one launch (start us, length us, event | category | flops | bytes accessed | tf_op | source)
XLA Modules:
  0.0 113.8 jit_solution(12400810134248172920)
XLA Ops:
  0.6 2.9 %shard_map.130 = (bf16[64,8,128]{2,1,0:T(8,128)(2,1)}, bf16[2,64,512]{2,1,0:T(8,128)(2,1)}) custom-call(s32[2,16,128]{2,1,0:T(8,128)} %bitcast.29, s32[2,128]{1,0:T(2,128)} %bitcast.34), custom_call_target="tpu_custom_call" | custom-call | tf_op jit(solution)/shard_map/pallas_call | solution.py:353
  3.5 12.0 %all-to-all-start = ((bf16[64,8,128]{2,1,0:T(8,128)(2,1)}), bf16[64,8,128]{2,1,0:T(8,128)(2,1)S(1)}, u32[]{:S(2)}, u32[]{:S(2)}) async-start(bf16[64,8,128]{2,1,0:T(8,128)(2,1)} %get-tuple-element.12), calls=%async_computation | async-start | bytes 262144 | tf_op jit(solution)/shard_map/all_to_all | solution.py:400
  15.5 0.0 copy-start.2
  15.5 1.2 %copy-done.2 = f32[512,2,256]{2,1,0:T(2,128)S(1)} copy-done((f32[512,2,256]{2,1,0:T(2,128)S(1)}, f32[512,2,256]{2,1,0:T(2,128)}, u32[]{:S(2)}) %copy-start.2) | copy-done | bytes 1048600
  16.7 0.1 shard_map.132.low_ref
  16.8 7.4 %all-to-all-done.code_ref = bf16[64,8,128]{2,1,0:T(8,128)(2,1)S(1)} async-done(((bf16[64,8,128]{2,1,0:T(8,128)(2,1)}), bf16[64,8,128]{2,1,0:T(8,128)(2,1)S(1)}, u32[]{:S(2)}, u32[]{:S(2)}) %all-to-all-start) | async-done | bytes 131104 | tf_op jit(solution)/shard_map/all_to_all | solution.py:400
  24.3 2.3 %shard_map.133 = bf16[64,64,256]{2,1,0:T(8,128)(2,1)} custom-call(bf16[64,8,128]{2,1,0:T(8,128)(2,1)S(1)} %all-to-all-done.code_ref, bf16[2,512,256]{2,1,0:T(8,128)(2,1)S(1)} %shard_map.132.low_ref), custom_call_target="tpu_custom_call" | custom-call | tf_op jit(solution)/shard_map/pallas_call | solution.py:353
  26.5 0.0 copy-start.11
  26.6 0.0 copy-start.4
  26.6 0.0 copy-start.6
  26.6 0.0 copy-start.7
  26.6 0.0 copy-start.9
  26.6 0.0 copy-start
  26.6 0.0 copy-start.5
  26.6 0.0 copy-start.10
  26.6 5.7 %all-to-all-start.1 = ((bf16[64,64,256]{2,1,0:T(8,128)(2,1)}), bf16[64,64,256]{2,1,0:T(8,128)(2,1)}, u32[]{:S(2)}, u32[]{:S(2)}) async-start(bf16[64,64,256]{2,1,0:T(8,128)(2,1)} %shard_map.133), calls=%async_computation.1 | async-start | bytes 4194304 | tf_op jit(solution)/shard_map/all_to_all | solution.py:421
  32.3 0.0 copy-done.11
  32.4 0.0 copy-done.4
  32.4 0.0 copy-done.6
  32.4 0.0 copy-done.7
  32.4 0.0 copy-done.9
  32.4 6.0 %shard_map.131.ct_ref = bf16[2,2048,128]{2,1,0:T(8,128)(2,1)S(1)} custom-call(s32[2,16,128]{2,1,0:T(8,128)S(1)} %bitcast.30, s32[2,128]{1,0:T(2,128)S(1)} %bitcast.35, bf16[2,16,128]{2,1,0:T(8,128)(2,1)S(1)} %bitcast.32, bf16[2,64,512]{2,1,0:T(8,128)(2,1)S(1)} %copy-done.4), custom_call_target="tpu_custom_call" | custom-call | tf_op jit(solution)/shard_map/pallas_call | solution.py:353
  38.4 21.3 %all-to-all-done.1.got_hbm = bf16[64,64,256]{2,1,0:T(8,128)(2,1)} async-done(((bf16[64,64,256]{2,1,0:T(8,128)(2,1)}), bf16[64,64,256]{2,1,0:T(8,128)(2,1)}, u32[]{:S(2)}, u32[]{:S(2)}) %all-to-all-start.1) | async-done | bytes 2097184 | tf_op jit(solution)/shard_map/all_to_all | solution.py:421
  59.8 0.0 copy-done
  59.8 0.0 copy-done.5
  59.8 0.0 copy-done.10
  59.8 9.0 %shard_map.134 = bf16[64,64,256]{2,1,0:T(8,128)(2,1)} custom-call(bf16[2,2048,128]{2,1,0:T(8,128)(2,1)S(1)} %shard_map.131.ct_ref, bf16[128,256]{1,0:T(8,128)(2,1)S(1)} %copy-done.5, s32[1,128]{1,0:T(1,128)S(1)} %bitcast.36, f32[1,4096]{1,0:T(1,128)S(1)} %bitcast.31, bf16[64,64,256]{2,1,0:T(8,128)(2,1)} %all-to-all-done.1.got_hbm, ...), custom_call_target="tpu_custom_call" | custom-call | tf_op jit(solution)/shard_map/pallas_call | solution.py:353
  68.8 0.0 copy-start.8
  68.8 6.7 %all-to-all-start.2 = ((bf16[64,64,256]{2,1,0:T(8,128)(2,1)}), bf16[64,64,256]{2,1,0:T(8,128)(2,1)S(1)}, u32[]{:S(2)}, u32[]{:S(2)}) async-start(bf16[64,64,256]{2,1,0:T(8,128)(2,1)} %shard_map.134), calls=%async_computation.2 | async-start | bytes 4194304 | tf_op jit(solution)/shard_map/all_to_all | solution.py:457
  75.5 0.0 copy-done.8
  75.5 3.0 %shard_map.135 = (f8e4m3fn[512,2048]{1,0:T(32,128)(4,1)S(1)}, f8e4m3fn[512,2048]{1,0:T(32,128)(4,1)}, f32[128,128]{1,0:T(8,128)S(1)}) custom-call(bf16[64,8,128]{2,1,0:T(8,128)(2,1)S(1)} %all-to-all-done.code_ref, f32[2,512]{1,0:T(2,128)S(1)} %bitcast.33), custom_call_target="tpu_custom_call" | custom-call | tf_op jit(solution)/shard_map/pallas_call | solution.py:353
  78.5 24.5 %all-to-all-done.2.share_ref = bf16[64,64,256]{2,1,0:T(8,128)(2,1)S(1)} async-done(((bf16[64,64,256]{2,1,0:T(8,128)(2,1)}), bf16[64,64,256]{2,1,0:T(8,128)(2,1)S(1)}, u32[]{:S(2)}, u32[]{:S(2)}) %all-to-all-start.2) | async-done | bytes 2097184 | tf_op jit(solution)/shard_map/all_to_all | solution.py:457
  103.0 0.0 copy-start.3
  103.0 1.2 %copy-done.3 = f8e4m3fn[512,2048]{1,0:T(32,128)(4,1)S(1)} copy-done((f8e4m3fn[512,2048]{1,0:T(32,128)(4,1)S(1)}, f8e4m3fn[512,2048]{1,0:T(32,128)(4,1)}, u32[]{:S(2)}) %copy-start.3) | copy-done | bytes 1048600
  104.2 1.0 shard_map.137.refs_1_
  105.2 0.0 copy-start.1
  105.2 3.4 %collective-permute-start.1 = (f32[640,256]{1,0:T(8,128)S(1)}, f32[640,256]{1,0:T(8,128)S(1)}, u32[]{:S(2)}, u32[]{:S(2)}) collective-permute-start(f32[640,256]{1,0:T(8,128)S(1)} %shard_map.137.refs_1_), channel_id=1, source_target_pairs={{0,64},{64,0},{1,65},{65,1},{2,66},{66,2},{3,67},{67,3},{4,68},{68... | collective-permute-start | bytes 1966088 | tf_op jit(solution)/shard_map/ppermute | solution.py:480
  108.6 1.0 shard_map.136.refs_0_
  109.6 0.1 collective-permute-start
  109.7 0.6 collective-permute-done.1.refs_3_
  110.4 1.5 %collective-permute-done.refs_2_ = f32[640,256]{1,0:T(8,128)S(1)} collective-permute-done((f32[640,256]{1,0:T(8,128)S(1)}, f32[640,256]{1,0:T(8,128)S(1)}, u32[]{:S(2)}, u32[]{:S(2)}) %collective-permute-start) | collective-permute-done | bytes 655392 | tf_op jit(solution)/shard_map/ppermute | solution.py:480
  111.8 0.0 copy-done.1
  111.8 2.0 %shard_map.138 = (f32[2048,128]{1,0:T(8,128)}, f32[2,512]{1,0:T(2,128)}, f32[2048,128]{1,0:T(8,128)}) custom-call(f32[640,256]{1,0:T(8,128)S(1)} %shard_map.136.refs_0_, f32[640,256]{1,0:T(8,128)S(1)} %shard_map.137.refs_1_, f32[640,256]{1,0:T(8,128)S(1)} %collective-permute-done.refs_2_, f32[640,256]{1,0:T(8,128)S(1)} %collective-permute-done.1.refs_3_, ...), custom_call_target="tpu_custom_call" | custom-call | tf_op jit(solution)/shard_map/pallas_call | solution.py:353
  (1 shorter events, 0.0 us)
Async XLA Ops:
  3.5 20.8 %all-to-all-start = ((bf16[64,8,128]{2,1,0:T(8,128)(2,1)}), bf16[64,8,128]{2,1,0:T(8,128)(2,1)S(1)}, u32[]{:S(2)}, u32[]{:S(2)}) async-start(bf16[64,8,128]{2,1,0:T(8,128)(2,1)} %get-tuple-element.12), calls=%async_computation | async-start | bytes 262144 | tf_op jit(solution)/shard_map/all_to_all | solution.py:400
  15.5 1.2 %copy-start.2 = (f32[512,2,256]{2,1,0:T(2,128)S(1)}, f32[512,2,256]{2,1,0:T(2,128)}, u32[]{:S(2)}) copy-start(f32[512,2,256]{2,1,0:T(2,128)} %param.16) | copy-start | bytes 3145732
  26.5 5.8 %copy-start.11 = (bf16[4096]{0:T(1024)(128)(2,1)S(1)}, bf16[4096]{0:T(1024)(128)(2,1)}, u32[]{:S(2)}) copy-start(bf16[4096]{0:T(1024)(128)(2,1)} %param.21) | copy-start | bytes 24580
  26.6 5.8 %copy-start.4 = (bf16[2,64,512]{2,1,0:T(8,128)(2,1)S(1)}, bf16[2,64,512]{2,1,0:T(8,128)(2,1)}, u32[]{:S(2)}) copy-start(bf16[2,64,512]{2,1,0:T(8,128)(2,1)} %get-tuple-element.13.rank_ref) | copy-start | bytes 393220
  26.6 5.8 %copy-start.6 = (s32[128,2,16]{0,2,1:T(8,128)S(1)}, s32[128,2,16]{0,2,1:T(8,128)}, u32[]{:S(2)}) copy-start(s32[128,2,16]{0,2,1:T(8,128)} %param.12) | copy-start | bytes 49156
  26.6 5.8 %copy-start.7 = (bf16[128,2,16]{0,2,1:T(8,128)(2,1)S(1)}, bf16[128,2,16]{0,2,1:T(8,128)(2,1)}, u32[]{:S(2)}) copy-start(bf16[128,2,16]{0,2,1:T(8,128)(2,1)} %param.14) | copy-start | bytes 24580
  26.6 5.8 %copy-start.9 = (s32[128,2]{0,1:T(2,128)S(1)}, s32[128,2]{0,1:T(2,128)}, u32[]{:S(2)}) copy-start(s32[128,2]{0,1:T(2,128)} %param.13) | copy-start | bytes 3076
  26.6 33.2 %copy-start = (bf16[768,768]{1,0:T(8,128)(2,1)S(1)}, bf16[768,768]{1,0:T(8,128)(2,1)}, u32[]{:S(2)}) copy-start(bf16[768,768]{1,0:T(8,128)(2,1)} %cross_hbm.1) | copy-start | bytes 3538948
  26.6 33.2 %copy-start.5 = (bf16[128,256]{1,0:T(8,128)(2,1)S(1)}, bf16[128,256]{1,0:T(8,128)(2,1)}, u32[]{:S(2)}) copy-start(bf16[128,256]{1,0:T(8,128)(2,1)} %dense_ref.1) | copy-start | bytes 196612
  26.6 33.1 %copy-start.10 = (s32[128]{0:T(128)S(1)}, s32[128]{0:T(128)}, u32[]{:S(2)}) copy-start(s32[128]{0:T(128)} %param.15) | copy-start | bytes 1540
  26.6 33.1 %all-to-all-start.1 = ((bf16[64,64,256]{2,1,0:T(8,128)(2,1)}), bf16[64,64,256]{2,1,0:T(8,128)(2,1)}, u32[]{:S(2)}, u32[]{:S(2)}) async-start(bf16[64,64,256]{2,1,0:T(8,128)(2,1)} %shard_map.133), calls=%async_computation.1 | async-start | bytes 4194304 | tf_op jit(solution)/shard_map/all_to_all | solution.py:421
  68.8 6.7 %copy-start.8 = (f32[512,2]{0,1:T(2,128)S(1)}, f32[512,2]{0,1:T(2,128)}, u32[]{:S(2)}) copy-start(f32[512,2]{0,1:T(2,128)} %param.18) | copy-start | bytes 12292
  68.8 34.2 %all-to-all-start.2 = ((bf16[64,64,256]{2,1,0:T(8,128)(2,1)}), bf16[64,64,256]{2,1,0:T(8,128)(2,1)S(1)}, u32[]{:S(2)}, u32[]{:S(2)}) async-start(bf16[64,64,256]{2,1,0:T(8,128)(2,1)} %shard_map.134), calls=%async_computation.2 | async-start | bytes 4194304 | tf_op jit(solution)/shard_map/all_to_all | solution.py:457
  103.0 1.2 %copy-start.3 = (f8e4m3fn[512,2048]{1,0:T(32,128)(4,1)S(1)}, f8e4m3fn[512,2048]{1,0:T(32,128)(4,1)}, u32[]{:S(2)}) copy-start(f8e4m3fn[512,2048]{1,0:T(32,128)(4,1)} %get-tuple-element.17.hot_ref) | copy-start | bytes 3145732
  105.2 6.6 %copy-start.1 = (f32[512,2,256]{2,1,0:T(2,128)S(1)}, f32[512,2,256]{2,1,0:T(2,128)}, u32[]{:S(2)}) copy-start(f32[512,2,256]{2,1,0:T(2,128)} %param.17) | copy-start | bytes 3145732
  105.2 5.1 %collective-permute-start.1 = (f32[640,256]{1,0:T(8,128)S(1)}, f32[640,256]{1,0:T(8,128)S(1)}, u32[]{:S(2)}, u32[]{:S(2)}) collective-permute-start(f32[640,256]{1,0:T(8,128)S(1)} %shard_map.137.refs_1_), channel_id=1, source_target_pairs={{0,64},{64,0},{1,65},{65,1},{2,66},{66,2},{3,67},{67,3},{4,68},{68... | collective-permute-start | bytes 1966088 | tf_op jit(solution)/shard_map/ppermute | solution.py:480
  109.6 2.2 %collective-permute-start = (f32[640,256]{1,0:T(8,128)S(1)}, f32[640,256]{1,0:T(8,128)S(1)}, u32[]{:S(2)}, u32[]{:S(2)}) collective-permute-start(f32[640,256]{1,0:T(8,128)S(1)} %shard_map.136.refs_0_), channel_id=1, source_target_pairs={{0,64},{64,0},{1,65},{65,1},{2,66},{66,2},{3,67},{67,3},{4,68},{68... | collective-permute-start | bytes 1966088 | tf_op jit(solution)/shard_map/ppermute | solution.py:480
